TPU v7x, 32 devices: a whole 2x2x4 slice. The times are simulated.
32 devices in a mesh: tm: 8 (over y, x, core), space: 4 (over z).
Axes of the slice: x: 2, y: 2, z: 4, core: 2. Of those that a mesh axis runs over, the one named last changes fastest.
Arguments:
- latents: float32 [8, 4, 32, 128], P('tm', None, 'space'), may hold values from -6 to 6
- owner_slot: int32 [1], replicated, may hold values from 0 to 7
- slot_steps: int32 [8], replicated, may hold values from 0 to 999
- step_table: float32 [1000], replicated, may hold values from 0.14 to 0.2
- mod_scale: float32 [1000, 320], replicated, may hold values from -3 to 3
- mod_shift: float32 [1000, 320], replicated, may hold values from -3 to 3
- w_in: bfloat16 [9, 320, 4], replicated, may hold values from -1 to 1
- w_one: bfloat16 [9, 320, 320], replicated, may hold values from -0.21875 to 0.21875
- w_two: bfloat16 [9, 320, 320], replicated, may hold values from -0.21875 to 0.21875
- w_out: bfloat16 [9, 4, 320], replicated, may hold values from -0.109375 to 0.109375
Outputs:
- iterates: float32 [8, 4, 32, 128], P('tm', None, 'space')
- window_end: float32 [4, 32, 128], P(None, 'space')
Inputs may be any that keep to these rules, and one draw needn't show every extreme that they name: `owner_slot`: the slot that holds the window's start latent.
All inputs are finite; a program needn't handle non-finite values.
Results may differ from a plain program's by a relative error of at most 0.013.
Values may be sent and summed in bfloat16 or wider, within the bound.
No kernel may reach another device: no remote copies, remote signals or barrier semaphores. Data moves between devices by JAX's collectives and lax.ppermute only.
A program may use at most 64 MiB of HBM per device.

v0:
```python
import functools

import jax
import jax.numpy as jnp
from jax import lax
from jax.experimental import pallas as pl
from jax.experimental.pallas import tpu as pltpu
from jax.sharding import PartitionSpec as P

ITERS = 3
HALO = 4
COLS = 128
F32, BF = jnp.float32, jnp.bfloat16
VMEM_SPEC = pl.BlockSpec(memory_space=pltpu.VMEM)
SMEM_SPEC = pl.BlockSpec(memory_space=pltpu.SMEM)
ANY_SPEC = pl.BlockSpec(memory_space=pl.ANY)


def silu(v):
    half = 0.5 * v
    return half + half * jnp.tanh(half)


def position(slot, owner, slots):
    return lax.rem(slot - owner + slots, slots)


def drift_kernel(first, slots, spaces, rows, owner_ref, steps_ref, table_ref, start_ref, sent_ref, scale_hbm, shift_hbm,
                 wi_ref, w1_hbm, w2_hbm, wo_ref, out_ref, w1, w2, mod, rem1, rem2, state, cols_in, keep, act_a, act_b,
                 acc, taps_out, wo, sems):
    chan = w1.shape[1]
    whole = chan // 256 * 256
    lat = out_ref.shape[0]
    slot, space = lax.axis_index("tm"), lax.axis_index("space")
    owner = owner_ref[0]
    t_step = steps_ref[slot]
    t_row = pl.multiple_of(t_step // 8 * 8, 8)
    copies = [
        pltpu.make_async_copy(scale_hbm.at[pl.ds(t_row, 8)], mod.at[0], sems.at[0]),
        pltpu.make_async_copy(shift_hbm.at[pl.ds(t_row, 8)], mod.at[1], sems.at[1]),
        pltpu.make_async_copy(w1_hbm, w1, sems.at[2]),
        pltpu.make_async_copy(w2_hbm, w2, sems.at[3]),
    ]
    for c in copies:
        c.start()
    lane = lax.broadcasted_iota(jnp.int32, (chan, COLS), 1)

    def inside(row):
        at = space * rows + row
        return jnp.where((at >= 0) & (at < spaces * rows), 1.0, 0.0).astype(F32)

    pieces = (
        (jnp.maximum(space - 1, 0), (rows - HALO) * COLS, HALO * COLS, 0, inside(-1)),
        (space, 0, rows * COLS, HALO * COLS, jnp.float32(1.0)),
        (jnp.minimum(space + 1, spaces - 1), 0, HALO * COLS, (rows + HALO) * COLS, inside(rows)),
    )
    for source, begin, width, put_at, weight in pieces:
        window = slice(begin, begin + width)
        if first:
            value = start_ref[slot, source, :, window].astype(F32)
        else:
            value = start_ref[owner, source, :, window].astype(F32)
            mine = position(slot, owner, slots)
            for q in range(slots):
                factor = jnp.where(position(q, owner, slots) < mine, table_ref[steps_ref[q]], 0.0)
                value = value + factor * sent_ref[q, source, :, window].astype(F32)
        state[:, put_at:put_at + width] = value.astype(BF).astype(F32) * weight

    def put(dst, row, v):
        dst[1, row] = v.astype(BF)
        dst[0, row] = jnp.where(lane == 0, 0.0, pltpu.roll(v, 1, 1)).astype(BF)
        dst[2, row] = jnp.where(lane == COLS - 1, 0.0, pltpu.roll(v, COLS - 1, 1)).astype(BF)

    n_in = rows + 6
    cols_in[...] = jnp.zeros_like(cols_in)
    lane4 = lax.broadcasted_iota(jnp.int32, (lat, COLS), 1)
    for r in range(rows + 2 * HALO):
        x = state[:, r * COLS:(r + 1) * COLS]
        shifted = (
            jnp.where(lane4 == 0, 0.0, pltpu.roll(x, 1, 1)),
            x,
            jnp.where(lane4 == COLS - 1, 0.0, pltpu.roll(x, COLS - 1, 1)),
        )
        for dr in range(3):
            if 0 <= r - dr < n_in:
                for dc in range(3):
                    k = (3 * dr + dc) * lat
                    cols_in[k:k + lat, (r - dr) * COLS:(r - dr + 1) * COLS] = shifted[dc]

    def first_layer(j, _):
        x = cols_in[:, pl.ds(pl.multiple_of(j * 256, 256), 256)].astype(BF)
        z = jnp.dot(wi_ref[...], x, preferred_element_type=F32).astype(BF)
        for h in range(2):
            zh = z[:, h * COLS:(h + 1) * COLS]
            row = 2 * j + h
            keep[row] = zh
            put(act_a, row, silu(zh.astype(F32)) * inside(row - 3))
        return 0

    lax.fori_loop(0, n_in // 2, first_layer, 0)

    def remainder(w):
        return jnp.concatenate([w[t, :, whole:] for t in range(9)], axis=1)

    def conv(src, w, rem, j):
        parts, total = [], None
        for t in range(9):
            dr, dc = t // 3, t % 3
            x = jnp.concatenate([src[dc, 2 * j + dr], src[dc, 2 * j + dr + 1]], axis=1)
            parts.append(x[whole:])
            p = jnp.dot(w[t, :, :whole], x[:whole], preferred_element_type=F32)
            total = p if total is None else total + p
        return total + jnp.dot(rem[...], jnp.concatenate(parts, axis=0), preferred_element_type=F32)

    def pipelined(src, w, rem, count, finish):
        acc[...] = conv(src, w, rem, 0)

        def step(j, _):
            new = conv(src, w, rem, j)
            finish(j - 1)
            acc[...] = new
            return 0

        lax.fori_loop(1, count, step, 0)
        finish(count - 1)

    def column(m):
        chosen = lax.broadcasted_iota(jnp.int32, (8, chan), 0) == lax.rem(t_step, 8)
        row = jnp.sum(jnp.where(chosen, m, 0.0), axis=0, keepdims=True)
        return jnp.transpose(jnp.broadcast_to(row, (8, chan)))[:, :1]

    copies[0].wait()
    copies[1].wait()
    scale, shift = 1.0 + column(mod[0]), column(mod[1])

    def finish_one(j):
        for h in range(2):
            row = 2 * j + h
            v = silu(acc[:, h * COLS:(h + 1) * COLS] * scale + shift)
            put(act_b, row, v * inside(row - 2))

    def finish_two(j):
        both = []
        for h in range(2):
            row = 2 * j + h
            second = (keep[row + 2].astype(F32) + acc[:, h * COLS:(h + 1) * COLS]).astype(BF).astype(F32)
            both.append((silu(second) * inside(row - 1)).astype(BF))
        taps_out[j] = jnp.dot(wo[...], jnp.concatenate(both, axis=1), preferred_element_type=F32)

    copies[2].wait()
    rem1[...] = remainder(w1)
    pipelined(act_a, w1, rem1, (rows + 4) // 2, finish_one)
    copies[3].wait()
    rem2[...] = remainder(w2)
    wo[...] = wo_ref[...]
    pipelined(act_b, w2, rem2, (rows + 2) // 2, finish_two)

    lane8 = lax.broadcasted_iota(jnp.int32, (8, COLS), 1)
    for r in range(rows):
        total = None
        for dr in range(3):
            q = r + dr
            p = taps_out[q // 2, :, (q % 2) * COLS:(q % 2 + 1) * COLS]
            for dc in range(3):
                t = 3 * dr + dc
                v = p[8 * t:8 * t + 8]
                if dc == 0:
                    v = jnp.where(lane8 == 0, 0.0, pltpu.roll(v, 1, 1))
                elif dc == 2:
                    v = jnp.where(lane8 == COLS - 1, 0.0, pltpu.roll(v, COLS - 1, 1))
                total = v if total is None else total + v
        out_ref[:, r * COLS:(r + 1) * COLS] = total[:lat].astype(BF)


def drift_call(first, slots, spaces, owner, steps, table, start, sent, scale, shift, wi, w1, w2, wo):
    chan, taps_k = wi.shape
    lat = start.shape[2]
    rows = start.shape[3] // COLS
    rest = 9 * (chan % 256)
    V = pltpu.VMEM
    return pl.pallas_call(
        functools.partial(drift_kernel, first, slots, spaces, rows),
        out_shape=jax.ShapeDtypeStruct((lat, rows * COLS), BF),
        in_specs=[SMEM_SPEC] * 3 + [VMEM_SPEC] * 2 + [ANY_SPEC] * 2 + [VMEM_SPEC, ANY_SPEC, ANY_SPEC, VMEM_SPEC],
        out_specs=VMEM_SPEC,
        scratch_shapes=[
            V(w1.shape, BF), V(w2.shape, BF), V((2, 8, chan), F32), V((chan, rest), BF), V((chan, rest), BF),
            V((lat, (rows + 8) * COLS), F32), V((taps_k, (rows + 6) * COLS), F32), V((rows + 6, chan, COLS), BF),
            V((3, rows + 6, chan, COLS), BF), V((3, rows + 4, chan, COLS), BF), V((chan, 256), F32),
            V(((rows + 2) // 2, wo.shape[0], 256), F32), V(wo.shape, BF), pltpu.SemaphoreType.DMA((4,)),
        ],
        compiler_params=pltpu.CompilerParams(vmem_limit_bytes=48 << 20),
        name="drift",
    )(owner, steps, table, start, sent, scale, shift, wi, w1, w2, wo)


def finish_kernel(slots, owner_ref, steps_ref, table_ref, got_ref, iterate_ref, end_ref):
    owner = owner_ref[0]
    mine = position(lax.axis_index("tm"), owner, slots)
    start = got_ref[owner, 1]
    lower, every = start, start
    for q in range(slots):
        size = table_ref[steps_ref[q]]
        drift = got_ref[q, 0]
        every = every + size * drift
        lower = lower + jnp.where(position(q, owner, slots) < mine, size, 0.0) * drift
    for r in range(iterate_ref.shape[2]):
        iterate_ref[0, :, r, :] = lower[:, r * COLS:(r + 1) * COLS]
        end_ref[:, r, :] = every[:, r * COLS:(r + 1) * COLS]


def to_everyone(value, axes, count):
    copies = jnp.broadcast_to(value[None], (count,) + value.shape)
    return lax.all_to_all(copies, axes, 0, 0)


def body(latents, owner_slot, slot_steps, step_table, mod_scale, mod_shift, w_in, w_one, w_two, w_out):
    slots, spaces = lax.axis_size("tm"), lax.axis_size("space")
    lat, rows = latents.shape[1], latents.shape[2]
    chan = w_one.shape[1]
    wi = jnp.pad(jnp.transpose(w_in, (1, 0, 2)).reshape(chan, 9 * lat), ((0, 0), (0, 48 - 9 * lat)))
    wo = jnp.pad(w_out, ((0, 0), (0, 8 - lat), (0, 0))).reshape(72, chan)
    flat = latents[0].reshape(lat, rows * COLS)

    def share(value):
        return to_everyone(value, ("tm", "space"), slots * spaces).reshape(slots, spaces, lat, rows * COLS)

    start = share(flat.astype(BF))
    sent = start
    for picard_step in range(ITERS):
        drift = drift_call(picard_step == 0, slots, spaces, owner_slot, slot_steps, step_table, start, sent,
                           mod_scale, mod_shift, wi, w_one, w_two, wo)
        if picard_step < ITERS - 1:
            sent = share(drift)
    got = to_everyone(jnp.stack([drift.astype(F32), flat]), "tm", slots)
    return pl.pallas_call(
        functools.partial(finish_kernel, slots),
        out_shape=(jax.ShapeDtypeStruct(latents.shape, F32), jax.ShapeDtypeStruct(latents.shape[1:], F32)),
        in_specs=[SMEM_SPEC] * 3 + [VMEM_SPEC],
        out_specs=(VMEM_SPEC, VMEM_SPEC),
        name="finish",
    )(owner_slot, slot_steps, step_table, got)


def solution(mesh):
    in_specs = (P("tm", None, "space", None), P(), P(), P(), P(), P(), P(), P(), P(), P())
    out_specs = (P("tm", None, "space", None), P(None, "space", None))
    return jax.shard_map(body, mesh=mesh, in_specs=in_specs, out_specs=out_specs, check_vma=False)
```

profile of v0, /device:TPU:0, one launch (start us, length us, event | category | flops | bytes accessed | tf_op | source)
XLA Modules:
  0.0 98.0 jit_solution(10397258557117869300)
XLA Ops:
  0.6 0.7 convert_bitcast_fusion
  1.4 0.8 broadcast_in_dim.8
  2.1 7.3 %all-to-all-start = ((bf16[32,4,1024]{2,1,0:T(4,128)(2,1)}), bf16[32,4,1024]{2,1,0:T(4,128)(2,1)S(1)}, u32[]{:S(2)}, u32[]{:S(2)}) async-start(bf16[32,4,1024]{2,1,0:T(4,128)(2,1)} %broadcast_in_dim.8), calls=%async_computation | async-start | bytes 524288 | tf_op jit(solution)/shard_map/all_to_all | solution.py:214
  10.1 1.8 %copy.20.scale_hbm = f32[1000,320]{1,0:T(8,128)S(1)} copy(f32[1000,320]{0,1:T(8,128)} %param.14) | data formatting | bytes 2560000 | tf_op args[4]
  11.9 0.0 copy-start.5
  11.9 0.0 copy-start.6
  11.9 0.0 copy-start.2
  11.9 0.0 copy-start.3
  11.9 1.8 %copy.21.shift_hbm = f32[1000,320]{1,0:T(8,128)S(1)} copy(f32[1000,320]{0,1:T(8,128)} %param.15) | data formatting | bytes 2560000 | tf_op args[5]
  13.7 0.0 copy-done.5
  13.8 0.1 copy.19
  13.9 0.0 copy-done.6
  14.0 5.7 %all-to-all-done = bf16[32,4,1024]{2,1,0:T(4,128)(2,1)S(1)} async-done(((bf16[32,4,1024]{2,1,0:T(4,128)(2,1)}), bf16[32,4,1024]{2,1,0:T(4,128)(2,1)S(1)}, u32[]{:S(2)}, u32[]{:S(2)}) %all-to-all-start) | async-done | bytes 262176 | tf_op jit(solution)/shard_map/all_to_all | solution.py:214
  19.6 0.0 copy-done.2
  19.6 0.0 copy-done.3
  19.7 0.0 copy-start
  19.7 1.6 %copy-done = bf16[9,320,320]{2,1,0:T(8,128)(2,1)S(1)} copy-done((bf16[9,320,320]{2,1,0:T(8,128)(2,1)S(1)}, bf16[9,320,320]{2,1,0:T(8,128)(2,1)}, u32[]{:S(2)}) %copy-start) | copy-done | bytes 1843224
  21.3 11.9 %drift.3 = bf16[4,1024]{1,0:T(4,128)(2,1)S(1)} custom-call(s32[1]{0:T(128)S(6)} %copy.29.owner_ref, s32[8]{0:T(128)S(1)} %copy-done.3, f32[1000]{0:T(1024)S(1)} %copy-done.2, bf16[8,4,4,1024]{3,2,1,0:T(4,128)(2,1)S(1)} %bitcast.19, bf16[8,4,4,1024]{3,2,1,0:T(4,128)(2,1)S(1)} %bitcast.20, f32[1000,320]{1,0:T(8,128)S(1)} %copy.20.scale_hbm, ...), custom_call_target="tpu_custom_call" | custom-call | tf_op jit(solution)/shard_map/drift/pallas_call | solution.py:181
  33.2 0.1 broadcast_in_dim.9
  33.3 12.7 %all_to_all.20 = bf16[32,4,1024]{2,1,0:T(4,128)(2,1)S(1)} all-to-all(bf16[32,4,1024]{2,1,0:T(4,128)(2,1)S(1)} %broadcast_in_dim.9), channel_id=1, replica_groups=mesh['tm'=8,'space'=4] {'tm','space'}, dimensions={0} | all-to-all | bytes 524288 | tf_op jit(solution)/shard_map/all_to_all | solution.py:214
  46.0 0.0 copy-start.4
  46.1 12.0 %drift.4 = bf16[4,1024]{1,0:T(4,128)(2,1)S(1)} custom-call(s32[1]{0:T(128)S(6)} %copy.29.owner_ref, s32[8]{0:T(128)S(1)} %copy-done.3, f32[1000]{0:T(1024)S(1)} %copy-done.2, bf16[8,4,4,1024]{3,2,1,0:T(4,128)(2,1)S(1)} %bitcast.21, bf16[8,4,4,1024]{3,2,1,0:T(4,128)(2,1)S(1)} %bitcast.23, f32[1000,320]{1,0:T(8,128)S(1)} %copy.20.scale_hbm, ...), custom_call_target="tpu_custom_call" | custom-call | tf_op jit(solution)/shard_map/drift/pallas_call | solution.py:181
  58.1 0.8 broadcast_in_dim.10
  58.8 3.3 %all-to-all-start.2 = ((bf16[32,4,1024]{2,1,0:T(4,128)(2,1)}), bf16[32,4,1024]{2,1,0:T(4,128)(2,1)}, u32[]{:S(2)}, u32[]{:S(2)}) async-start(bf16[32,4,1024]{2,1,0:T(4,128)(2,1)} %broadcast_in_dim.10), calls=%async_computation.2 | async-start | bytes 524288 | tf_op jit(solution)/shard_map/all_to_all | solution.py:214
  62.1 0.0 copy-done.4
  62.2 10.1 %all-to-all-done.2 = bf16[32,4,1024]{2,1,0:T(4,128)(2,1)} async-done(((bf16[32,4,1024]{2,1,0:T(4,128)(2,1)}), bf16[32,4,1024]{2,1,0:T(4,128)(2,1)}, u32[]{:S(2)}, u32[]{:S(2)}) %all-to-all-start.2) | async-done | bytes 262176 | tf_op jit(solution)/shard_map/all_to_all | solution.py:214
  72.3 0.0 copy-start.1
  72.3 1.6 %copy-done.1 = bf16[9,320,320]{2,1,0:T(8,128)(2,1)S(1)} copy-done((bf16[9,320,320]{2,1,0:T(8,128)(2,1)S(1)}, bf16[9,320,320]{2,1,0:T(8,128)(2,1)}, u32[]{:S(2)}) %copy-start.1) | copy-done | bytes 1843224
  73.9 12.4 %drift.5 = bf16[4,1024]{1,0:T(4,128)(2,1)S(1)} custom-call(s32[1]{0:T(128)S(6)} %copy.29.owner_ref, s32[8]{0:T(128)S(1)} %copy-done.3, f32[1000]{0:T(1024)S(1)} %copy-done.2, bf16[8,4,4,1024]{3,2,1,0:T(4,128)(2,1)S(1)} %bitcast.22, bf16[8,4,4,1024]{3,2,1,0:T(4,128)(2,1)} %bitcast.4.sent_ref, f32[1000,320]{1,0:T(8,128)S(1)} %copy.20.scale_hbm, ...), custom_call_target="tpu_custom_call" | custom-call | tf_op jit(solution)/shard_map/drift/pallas_call | solution.py:181
  86.4 10.0 %all_to_all.21.got_ref = f32[8,2,4,1024]{3,2,1,0:T(4,128)} all-to-all(f32[8,2,4,1024]{3,2,1,0:T(4,128)S(1)} %broadcast_in_dim.11), channel_id=1, replica_groups=mesh['tm'=8,'space'=4] {'tm'}, dimensions={0} | all-to-all | bytes 524288 | tf_op jit(solution)/shard_map/all_to_all | solution.py:214
  96.4 1.6 %finish.1 = (f32[1,4,8,128]{3,2,1,0:T(8,128)}, f32[4,8,128]{2,1,0:T(8,128)}) custom-call(s32[1]{0:T(128)S(6)} %copy.29.owner_ref, s32[8]{0:T(128)} %steps_ref.7, f32[1000]{0:T(1024)} %table_ref.7, f32[8,2,4,1024]{3,2,1,0:T(4,128)} %all_to_all.21.got_ref), custom_call_target="tpu_custom_call" | custom-call | tf_op jit(solution)/shard_map/finish/pallas_call | solution.py:236
  (8 shorter events, 0.1 us)
Async XLA Ops:
  2.1 17.5 %all-to-all-start = ((bf16[32,4,1024]{2,1,0:T(4,128)(2,1)}), bf16[32,4,1024]{2,1,0:T(4,128)(2,1)S(1)}, u32[]{:S(2)}, u32[]{:S(2)}) async-start(bf16[32,4,1024]{2,1,0:T(4,128)(2,1)} %broadcast_in_dim.8), calls=%async_computation | async-start | bytes 524288 | tf_op jit(solution)/shard_map/all_to_all | solution.py:214
  11.9 1.8 %copy-start.5 = (bf16[9,320,4]{1,2,0:T(4,128)(2,1)S(1)}, bf16[9,320,4]{1,2,0:T(4,128)(2,1)}, u32[]{:S(2)}) copy-start(bf16[9,320,4]{1,2,0:T(4,128)(2,1)} %param.16) | copy-start | bytes 69124
  11.9 2.0 %copy-start.6 = (bf16[9,4,320]{2,1,0:T(4,128)(2,1)S(1)}, bf16[9,4,320]{2,1,0:T(4,128)(2,1)}, u32[]{:S(2)}) copy-start(bf16[9,4,320]{2,1,0:T(4,128)(2,1)} %param.19) | copy-start | bytes 69124
  11.9 7.7 %copy-start.2 = (f32[1000]{0:T(1024)S(1)}, f32[1000]{0:T(1024)}, u32[]{:S(2)}) copy-start(f32[1000]{0:T(1024)} %table_ref.7) | copy-start | bytes 12004
  11.9 7.7 %copy-start.3 = (s32[8]{0:T(128)S(1)}, s32[8]{0:T(128)}, u32[]{:S(2)}) copy-start(s32[8]{0:T(128)} %steps_ref.7) | copy-start | bytes 100
  19.7 1.6 %copy-start = (bf16[9,320,320]{2,1,0:T(8,128)(2,1)S(1)}, bf16[9,320,320]{2,1,0:T(8,128)(2,1)}, u32[]{:S(2)}) copy-start(bf16[9,320,320]{2,1,0:T(8,128)(2,1)} %w1_hbm.5) | copy-start | bytes 5529604
  46.0 16.1 %copy-start.4 = (f32[1,4,8,128]{3,2,1,0:T(8,128)S(1)}, f32[1,4,8,128]{3,2,1,0:T(8,128)}, u32[]{:S(2)}) copy-start(f32[1,4,8,128]{3,2,1,0:T(8,128)} %param.10) | copy-start | bytes 49156
  58.8 13.5 %all-to-all-start.2 = ((bf16[32,4,1024]{2,1,0:T(4,128)(2,1)}), bf16[32,4,1024]{2,1,0:T(4,128)(2,1)}, u32[]{:S(2)}, u32[]{:S(2)}) async-start(bf16[32,4,1024]{2,1,0:T(4,128)(2,1)} %broadcast_in_dim.10), calls=%async_computation.2 | async-start | bytes 524288 | tf_op jit(solution)/shard_map/all_to_all | solution.py:214
  72.3 1.6 %copy-start.1 = (bf16[9,320,320]{2,1,0:T(8,128)(2,1)S(1)}, bf16[9,320,320]{2,1,0:T(8,128)(2,1)}, u32[]{:S(2)}) copy-start(bf16[9,320,320]{2,1,0:T(8,128)(2,1)} %w1_hbm.5) | copy-start | bytes 5529604
where the time goes:
time: 98.6 us; the launch traced here: 98 us
  Pallas kernels  37.9 us (38%)
  blocking collectives  22.8 us (23%)
  waiting for transfers between devices  15.8 us (16%)
  starting transfers between devices  10.6 us (11%)
  local copies, waits for them, and re-layouts  8.74 us (9%)
  between operations  1.45 us (1%)
    pallas_call x3, Pallas kernels, drift_call(): pl.pallas_call(functools.partial(drift_kernel, first, slots, spaces, rows...  36.3 us
    all_to_all x2, blocking collectives, to_everyone(): return lax.all_to_all(copies, axes, 0, 0)  22.8 us
    all_to_all x2, waiting for transfers between devices, to_everyone(): return lax.all_to_all(copies, axes, 0, 0)  15.8 us
    all_to_all x2, starting transfers between devices, to_everyone(): return lax.all_to_all(copies, axes, 0, 0)  10.6 us
    unnamed x17, local copies, waits for them, and re-layouts  6.85 us
  transfers between devices with their start and end apart: 2, of which 2 were waited for; matrix products, arithmetic and copies ran while one was open for 4% of the time, Pallas kernels for 0%

commit v1 on v0

v1 whole, which is shorter than its diff:
```python
import functools

import jax
import jax.numpy as jnp
from jax import lax
from jax.experimental import pallas as pl
from jax.experimental.pallas import tpu as pltpu
from jax.sharding import PartitionSpec as P

ITERS = 3
HALO = 4
COLS = 128
TAP_ROWS = 8
F32, BF = jnp.float32, jnp.bfloat16
VMEM_SPEC = pl.BlockSpec(memory_space=pltpu.VMEM)
SMEM_SPEC = pl.BlockSpec(memory_space=pltpu.SMEM)


def silu(v):
    half = 0.5 * v
    return half + half * jnp.tanh(half)


def position(slot, owner, slots):
    return lax.rem(slot - owner + slots, slots)


def factors_below(owner, steps_ref, table_ref, slot, slots):
    mine = position(slot, owner, slots)
    sizes = [jnp.where(position(q, owner, slots) < mine, table_ref[steps_ref[q]], 0.0) for q in range(slots)]
    return [jnp.where(owner == q, 1.0, sizes[q]) for q in range(slots)]


def weight_pieces(w, u):
    whole = w.shape[1] // 256 * 256
    rest = {}

    def piece(dc):
        top, mid, low = (w[3 * dr + dc].astype(F32) for dr in range(3))
        even, odd = 0.5 * (top + low), 0.5 * mid
        for i, v in enumerate((w[dc], (even + odd).astype(BF), (even - odd).astype(BF), w[6 + dc])):
            u[i, :, dc * whole:(dc + 1) * whole] = v[:, :whole]
            rest[i, dc] = v[:, whole:]
        if dc == 2:
            for i in range(4):
                u[i, :, 3 * whole:] = jnp.concatenate([rest[i, k] for k in range(3)], axis=1)

    return [functools.partial(piece, dc) for dc in range(3)]


def drift_kernel(first, last, copies, slots, spaces, rows, owner_ref, steps_ref, table_ref, own_ref, *refs):
    if first:
        (scale_hbm, shift_hbm, wi_in, wo_in, w1_hbm, w2_hbm, out_ref, *kept), refs = refs[:13], refs[13:]
        w1, w2, scale_all, shift_all, wi_rows, wo_rows, sems, *refs = refs
        loads = [pltpu.make_async_copy(src, dst, sems.at[n]) for n, (src, dst) in enumerate(
            ((w1_hbm, w1), (scale_hbm, scale_all), (shift_hbm, shift_all), (w2_hbm, w2)))]
        for load in loads:
            load.start()
    else:
        (sent_ref, *kept, out_ref), refs = refs[:8], refs[8:]
    scale_ref, shift_ref, wi_ref, wo_ref, u1, u2 = kept
    state, cols_in, keep, row_a, row_b, act_a, act_b, taps_out, prods = refs
    chan = scale_ref.shape[0]
    whole = chan // 256 * 256
    lat = out_ref.shape[-2]
    device_slot, space = lax.axis_index("tm"), lax.axis_index("space")
    owner = owner_ref[0]
    lane = lax.broadcasted_iota(jnp.int32, (chan, COLS), 1)

    def inside(row):
        at = space * rows + row
        return jnp.where((at >= 0) & (at < spaces * rows), 1.0, 0.0).astype(F32)

    before_one, beside_one = [], []
    if first:
        wi_rows[...] = jnp.zeros_like(wi_rows)
        wo_rows[...] = jnp.zeros_like(wo_rows)
        for t in range(9):
            wi_rows[t * lat:(t + 1) * lat, :chan] = wi_in[t].astype(F32)
            wo_rows[t * TAP_ROWS:t * TAP_ROWS + lat] = wo_in[t].astype(F32)
        wi_ref[...] = jnp.transpose(wi_rows[...])[:chan].astype(BF)
        wo_ref[...] = wo_rows[...].astype(BF)

        def modulation():
            t_step = steps_ref[device_slot]
            for load, src, dst, add in ((loads[1], scale_all, scale_ref, 1.0), (loads[2], shift_all, shift_ref, 0.0)):
                load.wait()
                chosen = lax.broadcasted_iota(jnp.int32, src.shape, 1) == t_step
                column = jnp.sum(jnp.where(chosen, src[...], 0.0), axis=1, keepdims=True)
                dst[...] = jnp.broadcast_to(column + add, dst.shape)

        before_one = [loads[0].wait] + weight_pieces(w1, u1)
        beside_one = [[modulation], [loads[3].wait] + weight_pieces(w2, u2)]

    if first:
        state[...] = own_ref[...].astype(BF).astype(F32)
    else:
        pieces = (
            (jnp.maximum(space - 1, 0), (rows - HALO) * COLS, HALO * COLS, 0, inside(-1)),
            (space, 0, rows * COLS, HALO * COLS, None),
            (jnp.minimum(space + 1, spaces - 1), 0, HALO * COLS, (rows + HALO) * COLS, inside(rows)),
        )
        factors = factors_below(owner, steps_ref, table_ref, device_slot, slots)
        for source, begin, width, put_at, weight in pieces:
            total = None
            for q in range(slots):
                term = factors[q] * sent_ref[q, source, :, begin:begin + width].astype(F32)
                total = term if total is None else total + term
            if weight is not None:
                total = total * weight
            value = jnp.where(device_slot == owner, own_ref[:, put_at:put_at + width], total)
            state[:, put_at:put_at + width] = value.astype(BF).astype(F32)

    n_in = rows + 6
    cols_in[...] = jnp.zeros_like(cols_in)
    lane4 = lax.broadcasted_iota(jnp.int32, (lat, COLS), 1)
    for r in range(rows + 2 * HALO):
        x = state[:, r * COLS:(r + 1) * COLS]
        shifted = (
            jnp.where(lane4 == 0, 0.0, pltpu.roll(x, 1, 1)),
            x,
            jnp.where(lane4 == COLS - 1, 0.0, pltpu.roll(x, COLS - 1, 1)),
        )
        for dr in range(3):
            if 0 <= r - dr < n_in:
                for dc in range(3):
                    k = (3 * dr + dc) * lat
                    cols_in[k:k + lat, (r - dr) * COLS:(r - dr + 1) * COLS] = shifted[dc]
    wi = wi_ref[:, :cols_in.shape[0]]

    def transformed(src, dst, p):
        r0, r1, r2, r3 = (src[2 * p + k] for k in range(4))
        for i, v in enumerate((r0 - r2, r1 + r2, r2 - r1, r1 - r3)):
            v = v.astype(BF)
            zero = jnp.zeros_like(v)
            dst[p, i, 1] = v
            dst[p, i, 0] = jnp.where(lane == 0, zero, pltpu.roll(v, 1, 1))
            dst[p, i, 2] = jnp.where(lane == COLS - 1, zero, pltpu.roll(v, COLS - 1, 1))

    def first_layer(j):
        x = cols_in[:, j * 256:(j + 1) * 256].astype(BF)
        z = jnp.dot(wi, x, preferred_element_type=F32).astype(BF)
        for h in range(2):
            zh = z[:, h * COLS:(h + 1) * COLS]
            row = 2 * j + h
            keep[row] = zh
            row_a[row] = silu(zh.astype(F32)) * inside(row - 3)
        if j:
            transformed(row_a, act_a, j - 1)

    def product(src, u, pairs, i):
        chunks = []
        for lo, hi in ((0, whole), (whole, chan)):
            for dc in range(3):
                chunks.append(jnp.concatenate([src[p, i, dc, lo:hi] for p in pairs], axis=1))
        return jnp.dot(u[i], jnp.concatenate(chunks, axis=0), preferred_element_type=F32)

    def conv(src, u, pairs, beside, slot):
        for i in range(4):
            prods[slot, i, :, :COLS * len(pairs)] = product(src, u, pairs, i)
            for work in beside[i * len(beside) // 4:(i + 1) * len(beside) // 4]:
                work()

    def untransformed(slot, row):
        at = slice(row // 2 * COLS, (row // 2 + 1) * COLS)
        if row % 2 == 0:
            return prods[slot, 0, :, at] + prods[slot, 1, :, at] + prods[slot, 2, :, at]
        return prods[slot, 1, :, at] - prods[slot, 2, :, at] - prods[slot, 3, :, at]

    def finish_one(row, slot, n):
        y = untransformed(slot, n)
        row_b[row] = silu(y * scale_ref[...] + shift_ref[...]) * inside(row - 2)
        if row >= 3 and row % 2:
            transformed(row_b, act_b, (row - 3) // 2)

    def finish_two(row, slot, n):
        y = untransformed(slot, n)
        second = (keep[row + 2].astype(F32) + y).astype(BF).astype(F32)
        act = (silu(second) * inside(row - 1)).astype(BF)
        taps_out[row] = jnp.dot(wo_ref[...], act, preferred_element_type=F32)

    pairs_one, pairs_two = (rows + 4) // 2, (rows + 2) // 2
    steps_one = [tuple(range(p, min(p + 2, pairs_one))) for p in range(0, pairs_one, 2)]
    steps_two = [tuple(range(p, min(p + 2, pairs_two))) for p in range(0, pairs_two, 2)]
    ready, slot = 0, 0
    waiting = []
    for pairs in steps_one:
        while ready <= pairs[-1] + 1:
            first_layer(ready)
            ready += 1
        for work in before_one:
            work()
        before_one = []
        beside = list(waiting)
        for j in range(ready, min(pairs[-1] + 4, pairs_one + 1)):
            beside.append(functools.partial(first_layer, j))
            ready = j + 1
        if beside_one:
            beside += beside_one.pop(0)
        conv(act_a, u1, pairs, beside, slot)
        waiting = [functools.partial(finish_one, 2 * pairs[0] + n, slot, n) for n in range(2 * len(pairs))]
        slot = 1 - slot
    done = 2 * steps_one[-1][0]
    for pairs in steps_two:
        if 2 * pairs[-1] + 3 >= done:
            for work in waiting:
                work()
            waiting, done = [], 2 * pairs_one
        conv(act_b, u2, pairs, waiting, slot)
        done = 2 * pairs_one
        waiting = [functools.partial(finish_two, 2 * pairs[0] + n, slot, n) for n in range(2 * len(pairs))]
        slot = 1 - slot
    for work in waiting:
        work()

    size = table_ref[steps_ref[device_slot]]
    lane8 = lax.broadcasted_iota(jnp.int32, (TAP_ROWS, COLS), 1)
    for r in range(rows):
        total = None
        for dc in range(3):
            v = None
            for dr in range(3):
                t = 3 * dr + dc
                p = taps_out[r + dr, TAP_ROWS * t:TAP_ROWS * (t + 1)]
                v = p if v is None else v + p
            if dc == 0:
                v = jnp.where(lane8 == 0, 0.0, pltpu.roll(v, 1, 1))
            elif dc == 2:
                v = jnp.where(lane8 == COLS - 1, 0.0, pltpu.roll(v, COLS - 1, 1))
            total = v if total is None else total + v
        drift = total[:lat].astype(BF).astype(F32)
        at = slice(r * COLS, (r + 1) * COLS)
        reached = own_ref[:, (r + HALO) * COLS:(r + HALO + 1) * COLS] + size * drift
        value = jnp.where(device_slot == owner, reached, drift)
        high = value.astype(BF)
        if last:
            low = (value - high.astype(F32)).astype(BF)
        for n in range(copies):
            if last:
                out_ref[n, 0, :, at] = high
                out_ref[n, 1, :, at] = low
            else:
                out_ref[n, :, at] = high


def drift_call(first, last, copies, slots, spaces, rows, chan, lat, tensors):
    V, S = pltpu.VMEM, jax.ShapeDtypeStruct
    hbm = pl.BlockSpec(memory_space=pltpu.HBM)
    padded = (chan + COLS - 1) // COLS * COLS
    outs = [S((copies, 2, lat, rows * COLS) if last else (copies, lat, rows * COLS), BF)]
    scratch = []
    specs = [SMEM_SPEC] * 3 + [VMEM_SPEC] * 8
    forms = [((chan, COLS), F32), ((chan, COLS), F32), ((chan, COLS), BF), ((9 * TAP_ROWS, chan), BF),
             ((4, chan, 3 * chan), BF), ((4, chan, 3 * chan), BF)]
    if first:
        specs = [SMEM_SPEC] * 3 + [VMEM_SPEC, hbm, hbm, VMEM_SPEC, VMEM_SPEC, hbm, hbm]
        outs += [V(*f) for f in forms]
        scratch = [V((9, chan, chan), BF), V((9, chan, chan), BF), V(tensors[4].shape, F32), V(tensors[5].shape, F32),
                   V((COLS, padded), F32), V((9 * TAP_ROWS, chan), F32), pltpu.SemaphoreType.DMA((4,))]
    scratch += [
        V((lat, (rows + 8) * COLS), F32), V((48, (rows + 6) * COLS), F32), V((rows + 6, chan, COLS), BF),
        V((rows + 6, chan, COLS), F32), V((rows + 4, chan, COLS), F32), V(((rows + 4) // 2, 4, 3, chan, COLS), BF),
        V(((rows + 2) // 2, 4, 3, chan, COLS), BF), V((rows + 2, 9 * TAP_ROWS, COLS), F32),
        V((2, 4, chan, 2 * COLS), F32),
    ]
    passes = 2 * chan * (3 * chan) * 2 * COLS * (rows + 4 + rows + 2)
    return pl.pallas_call(
        functools.partial(drift_kernel, first, last, copies, slots, spaces, rows),
        out_shape=outs,
        in_specs=specs,
        out_specs=[VMEM_SPEC] * len(outs),
        scratch_shapes=scratch,
        compiler_params=pltpu.CompilerParams(vmem_limit_bytes=(32 if first else 25) << 20),
        cost_estimate=pl.CostEstimate(flops=passes, transcendentals=36 * chan * COLS, bytes_accessed=6 << 20),
        name="drift",
    )(*tensors)


def finish_kernel(slots, owner_ref, steps_ref, table_ref, own_ref, sent_ref, iterate_ref, end_ref):
    owner = owner_ref[0]
    rows = iterate_ref.shape[2]
    slot = lax.axis_index("tm")
    below = factors_below(owner, steps_ref, table_ref, slot, slots)
    lower, every = None, None
    for q in range(slots):
        value = sent_ref[q, 0].astype(F32) + sent_ref[q, 1].astype(F32)
        low = below[q] * value
        full = jnp.where(owner == q, 1.0, table_ref[steps_ref[q]]) * value
        lower = low if lower is None else lower + low
        every = full if every is None else every + full
    lower = jnp.where(slot == owner, own_ref[:, HALO * COLS:(HALO + rows) * COLS], lower)
    for r in range(rows):
        iterate_ref[0, :, r, :] = lower[:, r * COLS:(r + 1) * COLS]
        end_ref[:, r, :] = every[:, r * COLS:(r + 1) * COLS]


def with_neighbour_rows(flat, width):
    count, index = lax.axis_size("space"), lax.axis_index("space")
    even = index % 2 == 0
    head, tail = flat[:, :width], flat[:, flat.shape[1] - width:]
    swap = lambda begin: [(i + a, i + 1 - a) for i in range(begin, count - 1, 2) for a in (0, 1)]
    one = lax.ppermute(jnp.where(even, tail, head), "space", swap(0))
    two = lax.ppermute(jnp.where(even, head, tail), "space", swap(1))
    return jnp.concatenate([jnp.where(even, two, one), flat, jnp.where(even, one, two)], axis=1)


def body(latents, owner_slot, slot_steps, step_table, mod_scale, mod_shift, w_in, w_one, w_two, w_out):
    slots, spaces = lax.axis_size("tm"), lax.axis_size("space")
    lat, rows = latents.shape[1], latents.shape[2]
    flat = latents[0].reshape(lat, rows * COLS)
    own = with_neighbour_rows(flat, HALO * COLS)
    call = functools.partial(drift_call, slots=slots, spaces=spaces, rows=rows, chan=w_one.shape[1], lat=lat)
    scalars = (owner_slot, slot_steps, step_table)
    everyone = slots * spaces
    stay = lambda a: pltpu.with_memory_space_constraint(a, pltpu.HBM)
    given = (stay(mod_scale.T), stay(mod_shift.T), jnp.transpose(w_in, (0, 2, 1)), w_out, stay(w_one), stay(w_two))
    drift, *weights = call(True, False, everyone, tensors=(*scalars, own, *given))
    for picard_step in range(1, ITERS):
        last = picard_step == ITERS - 1
        sent = lax.all_to_all(drift, ("tm", "space"), 0, 0).reshape(slots, spaces, lat, rows * COLS)
        drift, = call(False, last, slots if last else everyone, tensors=(*scalars, own, sent, *weights))
    sent = lax.all_to_all(drift, "tm", 0, 0)
    return pl.pallas_call(
        functools.partial(finish_kernel, slots),
        out_shape=(jax.ShapeDtypeStruct(latents.shape, F32), jax.ShapeDtypeStruct(latents.shape[1:], F32)),
        in_specs=[SMEM_SPEC] * 3 + [VMEM_SPEC] * 2,
        out_specs=(VMEM_SPEC, VMEM_SPEC),
        name="finish",
    )(*scalars, own, sent)


def solution(mesh):
    in_specs = (P("tm", None, "space", None), P(), P(), P(), P(), P(), P(), P(), P(), P())
    out_specs = (P("tm", None, "space", None), P(None, "space", None))
    return jax.shard_map(body, mesh=mesh, in_specs=in_specs, out_specs=out_specs, check_vma=False)
```

time: 98.6 us -> 75.4 us (0.76)
  waiting for transfers between devices: 15.8 us -> 0.97 us
  blocking collectives: 22.8 us -> 35.6 us
  Pallas kernels: 37.9 us -> 26.8 us
  local copies, waits for them, and re-layouts: 8.74 us -> 3.56 us
  starting transfers between devices: 10.6 us -> 6.57 us
    all_to_all x2 -> x0, waiting for transfers between devices: 15.8 us -> none  [to_everyone(): return lax.all_to_all(copies, axes, 0, 0)]
    all_to_all x2 -> x3, blocking collectives: 22.8 us -> 35.6 us  [the longest x2 27 us: body(): lax.all_to_all(drift, ('tm', 'space'), 0, 0)]
    pallas_call x3, Pallas kernels: 36.3 us -> 25.2 us  [drift_call(): pl.pallas_call(functools.partial(drift_kernel, first, last, copies, slots...]
    all_to_all x2 -> x0, starting transfers between devices: 10.6 us -> none  [to_everyone(): return lax.all_to_all(copies, axes, 0, 0)]
    ppermute x0 -> x2, starting transfers between devices: none -> 6.57 us  [the longest x1 5.91 us: with_neighbour_rows(): one = lax.ppermute(jnp.where(even, tail, head), 'space', swap(0))]
    unnamed x17 -> x11, local copies, waits for them, and re-layouts: 6.85 us -> 3.56 us
    broadcast_in_dim x4 -> x0, local copies, waits for them, and re-layouts: 1.67 us -> none  [to_everyone(): copies = jnp.broadcast_to(value[None], (count,) + value.shape)]
  transfers between devices with their start and end apart: 2 -> 2, of which waited for: 2 -> 1; matrix products, arithmetic and copies ran while one was open for 4% -> 0% of each run, Pallas kernels for 0% -> 0%
where the time goes in v1:
time: 75.4 us; the launch traced here: 74.9 us
  blocking collectives  35.6 us (47%)
  Pallas kernels  26.8 us (36%)
  starting transfers between devices  6.57 us (9%)
  local copies, waits for them, and re-layouts  3.56 us (5%)
  between operations  1.36 us (2%)
  waiting for transfers between devices  0.97 us (1%)
    all_to_all x2, blocking collectives, body(): lax.all_to_all(drift, ('tm', 'space'), 0, 0)  27 us
    pallas_call x3, Pallas kernels, drift_call(): pl.pallas_call(functools.partial(drift_kernel, first, last, copies, slots...  25.2 us
    all_to_all x1, blocking collectives, body(): sent = lax.all_to_all(drift, 'tm', 0, 0)  8.59 us
    ppermute x1, starting transfers between devices, with_neighbour_rows(): one = lax.ppermute(jnp.where(even, tail, head), 'space', swap(0))  5.91 us
    unnamed x11, local copies, waits for them, and re-layouts  3.56 us
    pallas_call x1, Pallas kernels, body(): pl.pallas_call(functools.partial(finish_kernel, slots), out_shape=(jax.Sh...  1.61 us
  transfers between devices with their start and end apart: 2, of which 1 were waited for; matrix products, arithmetic and copies ran while one was open for 0% of the time, Pallas kernels for 0%

profile of v1, /device:TPU:0, one launch (start us, length us, event | category | flops | bytes accessed | tf_op | source)
XLA Modules:
  0.0 74.9 jit_solution(3349838871217106546)
XLA Ops:
  0.6 0.7 copy.14
  1.4 0.7 collective-permute-start
  2.0 5.9 %collective-permute-start.1 = (f32[4,512]{1,0:T(4,128)S(1)}, f32[4,512]{1,0:T(4,128)S(1)}, u32[]{:S(2)}, u32[]{:S(2)}) collective-permute-start(f32[4,512]{1,0:T(4,128)S(1)} %get-tuple-element.19), channel_id=1, source_target_pairs={{0,1},{1,0},{2,3},{3,2},{4,5},{5,4},{6,7},{7,6},{8,9},{9,8},{10,11... | collective-permute-start | bytes 24584 | tf_op jit(solution)/shard_map/ppermute | solution.py:302
  8.6 0.0 collective-permute-done
  8.6 1.0 %collective-permute-done.1 = f32[4,512]{1,0:T(4,128)S(1)} collective-permute-done((f32[4,512]{1,0:T(4,128)S(1)}, f32[4,512]{1,0:T(4,128)S(1)}, u32[]{:S(2)}, u32[]{:S(2)}) %collective-permute-start.1) | collective-permute-done | bytes 8224 | tf_op jit(solution)/shard_map/ppermute | solution.py:302
  9.6 0.0 copy-start
  9.6 0.0 copy-start.1
  9.6 0.7 copy-done.1
  10.3 0.0 copy-start.2
  10.3 0.7 copy-done.2
  11.0 0.0 copy-start.3
  11.0 0.7 copy-done.3
  11.7 0.0 copy-start.4
  11.7 0.7 copy-done.4
  12.5 9.8 %drift.3 = (bf16[32,4,1024]{2,1,0:T(4,128)(2,1)S(1)}, f32[320,128]{1,0:T(8,128)S(1)}, f32[320,128]{1,0:T(8,128)S(1)}, bf16[320,128]{1,0:T(8,128)(2,1)S(1)}, bf16...) custom-call(s32[1]{0:T(128)S(6)} %copy.15.owner_ref, s32[8]{0:T(128)S(1)} %copy-done.2, ...), custom_call_target="tpu_custom_call" | custom-call | flops 3460300800 | bytes 6291456 | tf_op jit(solution)/shard_map/drift/pallas_call | solution.py:267
  22.3 14.3 %all_to_all.15 = bf16[32,4,1024]{2,1,0:T(4,128)(2,1)S(1)} all-to-all(bf16[32,4,1024]{2,1,0:T(4,128)(2,1)S(1)} %get-tuple-element.9), channel_id=1, replica_groups=mesh['tm'=8,'space'=4] {'tm','space'}, dimensions={0} | all-to-all | bytes 524288 | tf_op jit(solution)/shard_map/all_to_all | solution.py:320
  36.6 7.7 %drift.4 = bf16[32,4,1024]{2,1,0:T(4,128)(2,1)S(1)} custom-call(s32[1]{0:T(128)S(6)} %copy.15.owner_ref, s32[8]{0:T(128)S(1)} %copy-done.2, f32[1000]{0:T(1024)S(1)} %copy-done.1, f32[4,2048]{1,0:T(4,128)S(1)} %pad_maximum_fusion.own_ref, bf16[8,4,4,1024]{3,2,1,0:T(4,128)(2,1)S(1)} %bitcast.11, f32[320,128]{1,0:T(8,128)S(1)} %get-tuple-element.10.refs_1_, ...), custom_call_target="tpu_custom_call" | custom-call | flops 3460300800 | bytes 6291456 | tf_op jit(solution)/shard_map/drift/pallas_call | solution.py:267
  44.3 12.7 %all_to_all.16 = bf16[32,4,1024]{2,1,0:T(4,128)(2,1)S(1)} all-to-all(bf16[32,4,1024]{2,1,0:T(4,128)(2,1)S(1)} %drift.4), channel_id=1, replica_groups=mesh['tm'=8,'space'=4] {'tm','space'}, dimensions={0} | all-to-all | bytes 524288 | tf_op jit(solution)/shard_map/all_to_all | solution.py:320
  57.0 0.0 copy-done
  57.0 7.7 %drift.5 = bf16[8,2,4,1024]{3,2,1,0:T(4,128)(2,1)S(1)} custom-call(s32[1]{0:T(128)S(6)} %copy.15.owner_ref, s32[8]{0:T(128)S(1)} %copy-done.2, f32[1000]{0:T(1024)S(1)} %copy-done.1, f32[4,2048]{1,0:T(4,128)S(1)} %pad_maximum_fusion.own_ref, bf16[8,4,4,1024]{3,2,1,0:T(4,128)(2,1)S(1)} %bitcast.10, f32[320,128]{1,0:T(8,128)S(1)} %get-tuple-element.10.refs_1_, ...), custom_call_target="tpu_custom_call" | custom-call | flops 3460300800 | bytes 6291456 | tf_op jit(solution)/shard_map/drift/pallas_call | solution.py:267
  64.7 8.6 %all_to_all.17.sent_ref = bf16[8,2,4,1024]{3,2,1,0:T(4,128)(2,1)} all-to-all(bf16[8,2,4,1024]{3,2,1,0:T(4,128)(2,1)S(1)} %drift.5), channel_id=1, replica_groups=mesh['tm'=8,'space'=4] {'tm'}, dimensions={0} | all-to-all | bytes 262144 | tf_op jit(solution)/shard_map/all_to_all | solution.py:322
  73.3 1.6 %finish.1 = (f32[1,4,8,128]{3,2,1,0:T(8,128)}, f32[4,8,128]{2,1,0:T(8,128)}) custom-call(s32[1]{0:T(128)S(6)} %copy.15.owner_ref, s32[8]{0:T(128)} %steps_ref.7, f32[1000]{0:T(1024)} %table_ref.7, f32[4,2048]{1,0:T(4,128)} %copy-done, bf16[8,2,4,1024]{3,2,1,0:T(4,128)(2,1)} %all_to_all.17.sent_ref), custom_call_target="tpu_custom_call" | custom-call | tf_op jit(solution)/shard_map/finish/pallas_call | solution.py:323
  (3 shorter events, 0.0 us)
Async XLA Ops:
  1.4 7.2 %collective-permute-start = (f32[4,512]{1,0:T(4,128)S(1)}, f32[4,512]{1,0:T(4,128)S(1)}, u32[]{:S(2)}, u32[]{:S(2)}) collective-permute-start(f32[4,512]{1,0:T(4,128)S(1)} %get-tuple-element.18), channel_id=1, source_target_pairs={{1,2},{2,1},{5,6},{6,5},{9,10},{10,9},{13,14},{14,13},{17,18},{18,... | collective-permute-start | bytes 24584 | tf_op jit(solution)/shard_map/ppermute | solution.py:303
  2.0 7.5 %collective-permute-start.1 = (f32[4,512]{1,0:T(4,128)S(1)}, f32[4,512]{1,0:T(4,128)S(1)}, u32[]{:S(2)}, u32[]{:S(2)}) collective-permute-start(f32[4,512]{1,0:T(4,128)S(1)} %get-tuple-element.19), channel_id=1, source_target_pairs={{0,1},{1,0},{2,3},{3,2},{4,5},{5,4},{6,7},{7,6},{8,9},{9,8},{10,11... | collective-permute-start | bytes 24584 | tf_op jit(solution)/shard_map/ppermute | solution.py:302
  9.6 47.4 %copy-start = (f32[4,2048]{1,0:T(4,128)}, f32[4,2048]{1,0:T(4,128)S(1)}, u32[]{:S(2)}) copy-start(f32[4,2048]{1,0:T(4,128)S(1)} %pad_maximum_fusion.own_ref) | copy-start | bytes 98308
  9.6 0.7 copy-start.1
  10.3 0.7 copy-start.2
  11.0 0.7 copy-start.3
  11.7 0.7 copy-start.4

commit v2 on v1

--- a/solution.py
+++ b/solution.py
@@ -16,8 +16,7 @@
 SMEM_SPEC = pl.BlockSpec(memory_space=pltpu.SMEM)
 
 
-def silu(v):
-    half = 0.5 * v
+def silu(half):
     return half + half * jnp.tanh(half)
 
 
@@ -25,10 +24,24 @@
     return lax.rem(slot - owner + slots, slots)
 
 
-def factors_below(owner, steps_ref, table_ref, slot, slots):
+def write_factors(out, owner_ref, steps_ref, table_ref, slot, slots):
+    owner = owner_ref[0]
     mine = position(slot, owner, slots)
-    sizes = [jnp.where(position(q, owner, slots) < mine, table_ref[steps_ref[q]], 0.0) for q in range(slots)]
-    return [jnp.where(owner == q, 1.0, sizes[q]) for q in range(slots)]
+    owns = slot == owner
+    values = []
+    for q in range(slots):
+        size = table_ref[steps_ref[q]]
+        below = jnp.where(position(q, owner, slots) < mine, size, 0.0)
+        values.append(jnp.where(owns, 0.0, jnp.where(owner == q, 1.0, below)))
+    values += [jnp.where(owner == q, 1.0, table_ref[steps_ref[q]]) for q in range(slots)]
+    one = jnp.where(owns, 1.0, 0.0)
+    values += [one, jnp.where(owns, table_ref[steps_ref[slot]], 1.0), one]
+    for n, value in enumerate(values):
+        out[n] = jnp.full(out.shape[1:], value, F32)
+
+
+def start_rows(space, if_even, if_odd):
+    return [jnp.where(lax.rem(space, 2) == 0, if_even[:, k], if_odd[:, k]) for k in range(HALO)]
 
 
 def weight_pieces(w, u):
@@ -48,33 +61,37 @@
     return [functools.partial(piece, dc) for dc in range(3)]
 
 
-def drift_kernel(first, last, copies, slots, spaces, rows, owner_ref, steps_ref, table_ref, own_ref, *refs):
+def drift_kernel(first, last, copies, slots, spaces, rows, sent_one, sent_two, got_one, got_two, *refs):
     if first:
-        (scale_hbm, shift_hbm, wi_in, wo_in, w1_hbm, w2_hbm, out_ref, *kept), refs = refs[:13], refs[13:]
-        w1, w2, scale_all, shift_all, wi_rows, wo_rows, sems, *refs = refs
+        (owner_ref, steps_ref, table_ref, scale_hbm, shift_hbm, wi_hbm, wo_hbm, w1_hbm, w2_hbm, out_ref, *kept) = refs[:17]
+        (w1, w2, scale_all, shift_all, wi_in, wo_in, wi_rows, wo_rows, sems, *refs) = refs[17:]
         loads = [pltpu.make_async_copy(src, dst, sems.at[n]) for n, (src, dst) in enumerate(
-            ((w1_hbm, w1), (scale_hbm, scale_all), (shift_hbm, shift_all), (w2_hbm, w2)))]
+            ((wi_hbm, wi_in), (wo_hbm, wo_in), (w1_hbm, w1), (scale_hbm, scale_all), (shift_hbm, shift_all), (w2_hbm, w2)))]
         for load in loads:
             load.start()
     else:
-        (sent_ref, *kept, out_ref), refs = refs[:8], refs[8:]
-    scale_ref, shift_ref, wi_ref, wo_ref, u1, u2 = kept
+        (sent_ref, *kept, out_ref), refs = refs[:9], refs[9:]
+    scale_ref, shift_ref, wi_ref, wo_ref, factors, u1, u2 = kept
     state, cols_in, keep, row_a, row_b, act_a, act_b, taps_out, prods = refs
     chan = scale_ref.shape[0]
     whole = chan // 256 * 256
     lat = out_ref.shape[-2]
     device_slot, space = lax.axis_index("tm"), lax.axis_index("space")
-    owner = owner_ref[0]
     lane = lax.broadcasted_iota(jnp.int32, (chan, COLS), 1)
 
-    def inside(row):
+    def masked(v, row):
+        if 0 <= row < rows:
+            return v
         at = space * rows + row
-        return jnp.where((at >= 0) & (at < spaces * rows), 1.0, 0.0).astype(F32)
+        return v * jnp.where((at >= 0) & (at < spaces * rows), 1.0, 0.0).astype(F32)
 
     before_one, beside_one = [], []
     if first:
         wi_rows[...] = jnp.zeros_like(wi_rows)
         wo_rows[...] = jnp.zeros_like(wo_rows)
+        write_factors(factors, owner_ref, steps_ref, table_ref, device_slot, slots)
+        loads[0].wait()
+        loads[1].wait()
         for t in range(9):
             wi_rows[t * lat:(t + 1) * lat, :chan] = wi_in[t].astype(F32)
             wo_rows[t * TAP_ROWS:t * TAP_ROWS + lat] = wo_in[t].astype(F32)
@@ -83,33 +100,34 @@
 
         def modulation():
             t_step = steps_ref[device_slot]
-            for load, src, dst, add in ((loads[1], scale_all, scale_ref, 1.0), (loads[2], shift_all, shift_ref, 0.0)):
-                load.wait()
+            loads[3].wait()
+            loads[4].wait()
+            for src, dst, add in ((scale_all, scale_ref, 1.0), (shift_all, shift_ref, 0.0)):
                 chosen = lax.broadcasted_iota(jnp.int32, src.shape, 1) == t_step
                 column = jnp.sum(jnp.where(chosen, src[...], 0.0), axis=1, keepdims=True)
-                dst[...] = jnp.broadcast_to(column + add, dst.shape)
-
-        before_one = [loads[0].wait] + weight_pieces(w1, u1)
-        beside_one = [[modulation], [loads[3].wait] + weight_pieces(w2, u2)]
-
-    if first:
-        state[...] = own_ref[...].astype(BF).astype(F32)
-    else:
-        pieces = (
-            (jnp.maximum(space - 1, 0), (rows - HALO) * COLS, HALO * COLS, 0, inside(-1)),
-            (space, 0, rows * COLS, HALO * COLS, None),
-            (jnp.minimum(space + 1, spaces - 1), 0, HALO * COLS, (rows + HALO) * COLS, inside(rows)),
-        )
-        factors = factors_below(owner, steps_ref, table_ref, device_slot, slots)
-        for source, begin, width, put_at, weight in pieces:
+                dst[...] = jnp.broadcast_to(0.5 * (column + add), dst.shape)
+
+        before_one = [loads[2].wait] + weight_pieces(w1, u1)
+        beside_one = [[modulation], [], [loads[5].wait] + weight_pieces(w2, u2)]
+
+    own_rows = start_rows(space, got_two, got_one) + start_rows(space, sent_two, sent_one)
+    own_rows += start_rows(space, sent_one, sent_two) + start_rows(space, got_one, got_two)
+    for k, own in enumerate(own_rows):
+        value = own
+        if not first:
+            row = k - HALO
+            source = space
+            if row < 0:
+                source = jnp.maximum(space - 1, 0)
+            elif row >= rows:
+                source = jnp.minimum(space + 1, spaces - 1)
+            at = slice(row % rows * COLS, (row % rows + 1) * COLS)
             total = None
             for q in range(slots):
-                term = factors[q] * sent_ref[q, source, :, begin:begin + width].astype(F32)
+                term = factors[q, :lat] * sent_ref[q, source, :, at].astype(F32)
                 total = term if total is None else total + term
-            if weight is not None:
-                total = total * weight
-            value = jnp.where(device_slot == owner, own_ref[:, put_at:put_at + width], total)
-            state[:, put_at:put_at + width] = value.astype(BF).astype(F32)
+            value = masked(total, row) + factors[2 * slots, :lat] * own
+        state[:, k * COLS:(k + 1) * COLS] = value.astype(BF).astype(F32)
 
     n_in = rows + 6
     cols_in[...] = jnp.zeros_like(cols_in)
@@ -144,7 +162,7 @@
             zh = z[:, h * COLS:(h + 1) * COLS]
             row = 2 * j + h
             keep[row] = zh
-            row_a[row] = silu(zh.astype(F32)) * inside(row - 3)
+            row_a[row] = masked(silu(0.5 * zh.astype(F32)), row - 3)
         if j:
             transformed(row_a, act_a, j - 1)
 
@@ -169,14 +187,14 @@
 
     def finish_one(row, slot, n):
         y = untransformed(slot, n)
-        row_b[row] = silu(y * scale_ref[...] + shift_ref[...]) * inside(row - 2)
+        row_b[row] = masked(silu(y * scale_ref[...] + shift_ref[...]), row - 2)
         if row >= 3 and row % 2:
             transformed(row_b, act_b, (row - 3) // 2)
 
     def finish_two(row, slot, n):
         y = untransformed(slot, n)
         second = (keep[row + 2].astype(F32) + y).astype(BF).astype(F32)
-        act = (silu(second) * inside(row - 1)).astype(BF)
+        act = masked(silu(0.5 * second), row - 1).astype(BF)
         taps_out[row] = jnp.dot(wo_ref[...], act, preferred_element_type=F32)
 
     pairs_one, pairs_two = (rows + 4) // 2, (rows + 2) // 2
@@ -213,7 +231,6 @@
     for work in waiting:
         work()
 
-    size = table_ref[steps_ref[device_slot]]
     lane8 = lax.broadcasted_iota(jnp.int32, (TAP_ROWS, COLS), 1)
     for r in range(rows):
         total = None
@@ -230,8 +247,7 @@
             total = v if total is None else total + v
         drift = total[:lat].astype(BF).astype(F32)
         at = slice(r * COLS, (r + 1) * COLS)
-        reached = own_ref[:, (r + HALO) * COLS:(r + HALO + 1) * COLS] + size * drift
-        value = jnp.where(device_slot == owner, reached, drift)
+        value = factors[2 * slots + 1, :lat] * drift + factors[2 * slots + 2, :lat] * own_rows[HALO + r]
         high = value.astype(BF)
         if last:
             low = (value - high.astype(F32)).astype(BF)
@@ -249,14 +265,14 @@
     padded = (chan + COLS - 1) // COLS * COLS
     outs = [S((copies, 2, lat, rows * COLS) if last else (copies, lat, rows * COLS), BF)]
     scratch = []
-    specs = [SMEM_SPEC] * 3 + [VMEM_SPEC] * 8
-    forms = [((chan, COLS), F32), ((chan, COLS), F32), ((chan, COLS), BF), ((9 * TAP_ROWS, chan), BF),
-             ((4, chan, 3 * chan), BF), ((4, chan, 3 * chan), BF)]
+    specs = [VMEM_SPEC] * 12
     if first:
-        specs = [SMEM_SPEC] * 3 + [VMEM_SPEC, hbm, hbm, VMEM_SPEC, VMEM_SPEC, hbm, hbm]
-        outs += [V(*f) for f in forms]
-        scratch = [V((9, chan, chan), BF), V((9, chan, chan), BF), V(tensors[4].shape, F32), V(tensors[5].shape, F32),
-                   V((COLS, padded), F32), V((9 * TAP_ROWS, chan), F32), pltpu.SemaphoreType.DMA((4,))]
+        specs = [VMEM_SPEC] * 4 + [SMEM_SPEC] * 3 + [hbm] * 6
+        outs += [V((chan, COLS), F32), V((chan, COLS), F32), V((chan, COLS), BF), V((9 * TAP_ROWS, chan), BF),
+                 V((2 * slots + 3, 8, COLS), F32), V((4, chan, 3 * chan), BF), V((4, chan, 3 * chan), BF)]
+        scratch = [V((9, chan, chan), BF), V((9, chan, chan), BF), V(tensors[7].shape, F32), V(tensors[8].shape, F32),
+                   V(tensors[9].shape, BF), V(tensors[10].shape, BF), V((COLS, padded), F32),
+                   V((9 * TAP_ROWS, chan), F32), pltpu.SemaphoreType.DMA((6,))]
     scratch += [
         V((lat, (rows + 8) * COLS), F32), V((48, (rows + 6) * COLS), F32), V((rows + 6, chan, COLS), BF),
         V((rows + 6, chan, COLS), F32), V((rows + 4, chan, COLS), F32), V(((rows + 4) // 2, 4, 3, chan, COLS), BF),
@@ -276,57 +292,55 @@
     )(*tensors)
 
 
-def finish_kernel(slots, owner_ref, steps_ref, table_ref, own_ref, sent_ref, iterate_ref, end_ref):
-    owner = owner_ref[0]
-    rows = iterate_ref.shape[2]
-    slot = lax.axis_index("tm")
-    below = factors_below(owner, steps_ref, table_ref, slot, slots)
-    lower, every = None, None
-    for q in range(slots):
-        value = sent_ref[q, 0].astype(F32) + sent_ref[q, 1].astype(F32)
-        low = below[q] * value
-        full = jnp.where(owner == q, 1.0, table_ref[steps_ref[q]]) * value
-        lower = low if lower is None else lower + low
-        every = full if every is None else every + full
-    lower = jnp.where(slot == owner, own_ref[:, HALO * COLS:(HALO + rows) * COLS], lower)
+def finish_kernel(slots, sent_one, sent_two, sent_ref, factors, iterate_ref, end_ref):
+    rows, lat = iterate_ref.shape[2], iterate_ref.shape[1]
+    space = lax.axis_index("space")
+    own_rows = start_rows(space, sent_two, sent_one) + start_rows(space, sent_one, sent_two)
     for r in range(rows):
-        iterate_ref[0, :, r, :] = lower[:, r * COLS:(r + 1) * COLS]
-        end_ref[:, r, :] = every[:, r * COLS:(r + 1) * COLS]
-
-
-def with_neighbour_rows(flat, width):
+        at = slice(r * COLS, (r + 1) * COLS)
+        lower, every = factors[2 * slots, :lat] * own_rows[r], None
+        for q in range(slots):
+            value = sent_ref[q, 0, :, at].astype(F32) + sent_ref[q, 1, :, at].astype(F32)
+            full = factors[slots + q, :lat] * value
+            lower = lower + factors[q, :lat] * value
+            every = full if every is None else every + full
+        iterate_ref[0, :, r, :] = lower
+        end_ref[:, r, :] = every
+
+
+def neighbour_rows(rows):
     count, index = lax.axis_size("space"), lax.axis_index("space")
     even = index % 2 == 0
-    head, tail = flat[:, :width], flat[:, flat.shape[1] - width:]
+    head, tail = rows[:, :HALO], rows[:, rows.shape[1] - HALO:]
     swap = lambda begin: [(i + a, i + 1 - a) for i in range(begin, count - 1, 2) for a in (0, 1)]
-    one = lax.ppermute(jnp.where(even, tail, head), "space", swap(0))
-    two = lax.ppermute(jnp.where(even, head, tail), "space", swap(1))
-    return jnp.concatenate([jnp.where(even, two, one), flat, jnp.where(even, one, two)], axis=1)
+    one, two = jnp.where(even, tail, head), jnp.where(even, head, tail)
+    return one, two, lax.ppermute(one, "space", swap(0)), lax.ppermute(two, "space", swap(1))
 
 
 def body(latents, owner_slot, slot_steps, step_table, mod_scale, mod_shift, w_in, w_one, w_two, w_out):
     slots, spaces = lax.axis_size("tm"), lax.axis_size("space")
     lat, rows = latents.shape[1], latents.shape[2]
-    flat = latents[0].reshape(lat, rows * COLS)
-    own = with_neighbour_rows(flat, HALO * COLS)
+    assert rows == 2 * HALO
+    state = neighbour_rows(latents[0])
     call = functools.partial(drift_call, slots=slots, spaces=spaces, rows=rows, chan=w_one.shape[1], lat=lat)
-    scalars = (owner_slot, slot_steps, step_table)
     everyone = slots * spaces
     stay = lambda a: pltpu.with_memory_space_constraint(a, pltpu.HBM)
-    given = (stay(mod_scale.T), stay(mod_shift.T), jnp.transpose(w_in, (0, 2, 1)), w_out, stay(w_one), stay(w_two))
-    drift, *weights = call(True, False, everyone, tensors=(*scalars, own, *given))
+    given = (mod_scale.T, mod_shift.T, jnp.transpose(w_in, (0, 2, 1)), w_out, w_one, w_two)
+    drift, *weights = call(True, False, everyone, tensors=(
+        *state, owner_slot, stay(slot_steps), stay(step_table), *(stay(a) for a in given)))
     for picard_step in range(1, ITERS):
         last = picard_step == ITERS - 1
         sent = lax.all_to_all(drift, ("tm", "space"), 0, 0).reshape(slots, spaces, lat, rows * COLS)
-        drift, = call(False, last, slots if last else everyone, tensors=(*scalars, own, sent, *weights))
+        drift, = call(False, last, slots if last else everyone, tensors=(*state, sent, *weights))
     sent = lax.all_to_all(drift, "tm", 0, 0)
     return pl.pallas_call(
         functools.partial(finish_kernel, slots),
         out_shape=(jax.ShapeDtypeStruct(latents.shape, F32), jax.ShapeDtypeStruct(latents.shape[1:], F32)),
-        in_specs=[SMEM_SPEC] * 3 + [VMEM_SPEC] * 2,
+        in_specs=[VMEM_SPEC] * 4,
         out_specs=(VMEM_SPEC, VMEM_SPEC),
+        compiler_params=pltpu.CompilerParams(vmem_limit_bytes=4 << 20),
         name="finish",
-    )(*scalars, own, sent)
+    )(*state[:2], sent, weights[4])
 
 
 def solution(mesh):

time: 75.4 us -> 69.2 us (0.918)
  local copies, waits for them, and re-layouts: 3.56 us -> 0 us
  Pallas kernels: 26.8 us -> 24.1 us
  other arithmetic: 0.02 us -> 0.8 us
    unnamed x11 -> x0, local copies, waits for them, and re-layouts: 3.56 us -> none
    pallas_call x3, Pallas kernels: 25.2 us -> 23.4 us  [drift_call(): pl.pallas_call(functools.partial(drift_kernel, first, last, copies, slots...]
    pallas_call x1, Pallas kernels: 1.61 us -> 0.71 us  [body(): pl.pallas_call(functools.partial(finish_kernel, slots), out_shape=(jax.Sh...]
    select_n x2 -> x1, other arithmetic: 0.01 us -> 0.8 us  [neighbour_rows(): one, two = (jnp.where(even, tail, head), jnp.where(even, head, tail))]
where the time goes in v2:
time: 69.2 us; the launch traced here: 68.7 us
  blocking collectives  34.9 us (50%)
  Pallas kernels  24.1 us (35%)
  starting transfers between devices  6.56 us (9%)
  between operations  1.33 us (2%)
  waiting for transfers between devices  0.97 us (1%)
  other arithmetic  0.8 us (1%)
    all_to_all x2, blocking collectives, body(): lax.all_to_all(drift, ('tm', 'space'), 0, 0)  27 us
    pallas_call x3, Pallas kernels, drift_call(): pl.pallas_call(functools.partial(drift_kernel, first, last, copies, slots...  23.4 us
    all_to_all x1, blocking collectives, body(): sent = lax.all_to_all(drift, 'tm', 0, 0)  7.92 us
    ppermute x1, starting transfers between devices, neighbour_rows(): lax.ppermute(one, 'space', swap(0))  5.91 us
  transfers between devices with their start and end apart: 2, of which 1 were waited for; matrix products, arithmetic and copies ran while one was open for 0% of the time, Pallas kernels for 0%

profile of v2, /device:TPU:0, one launch (start us, length us, event | category | flops | bytes accessed | tf_op | source)
XLA Modules:
  0.0 68.7 jit_solution(9788368493466922637)
XLA Ops:
  0.6 0.8 %slice_select_fusion = (f32[4,4,128]{2,1,0:T(4,128)S(1)}, f32[4,4,128]{2,1,0:T(4,128)S(1)}) fusion(f32[4,8,128]{2,1,0:T(8,128)} %bitcast.8, pred[]{:T(512)S(6)} %eq.5), kind=kLoop, calls=%fused_computation | loop fusion | flops 4096 | bytes 32769 | tf_op jit(solution)/shard_map/jit(_where)/select_n | solution.py:316
  1.4 0.6 collective-permute-start.1
  2.1 5.9 %collective-permute-start = (f32[4,4,128]{2,1,0:T(4,128)S(1)}, f32[4,4,128]{2,1,0:T(4,128)S(1)}, u32[]{:S(2)}, u32[]{:S(2)}) collective-permute-start(f32[4,4,128]{2,1,0:T(4,128)S(1)} %get-tuple-element.19.sent_one), channel_id=1, source_target_pairs={{0,1},{1,0},{2,3},{3,2},{4,5},{5,4},{6,7},{7,6},{8,9},{9,8},{10,11... | collective-permute-start | bytes 24584 | tf_op jit(solution)/shard_map/ppermute | solution.py:317
  8.7 0.0 collective-permute-done.1.got_two
  8.7 1.0 %collective-permute-done.got_one = f32[4,4,128]{2,1,0:T(4,128)S(1)} collective-permute-done((f32[4,4,128]{2,1,0:T(4,128)S(1)}, f32[4,4,128]{2,1,0:T(4,128)S(1)}, u32[]{:S(2)}, u32[]{:S(2)}) %collective-permute-start) | collective-permute-done | bytes 8224 | tf_op jit(solution)/shard_map/ppermute | solution.py:317
  9.6 9.7 %drift.3 = (bf16[32,4,1024]{2,1,0:T(4,128)(2,1)S(1)}, f32[320,128]{1,0:T(8,128)S(1)}, f32[320,128]{1,0:T(8,128)S(1)}, bf16[320,128]{1,0:T(8,128)(2,1)S(1)}, bf16...) custom-call(f32[4,4,128]{2,1,0:T(4,128)S(1)} %get-tuple-element.19.s, ...), custom_call_target="tpu_custom_call" | custom-call | flops 3460300800 | bytes 6291456 | tf_op jit(solution)/shard_map/drift/pallas_call | solution.py:283
  19.4 14.3 %all_to_all.15 = bf16[32,4,1024]{2,1,0:T(4,128)(2,1)S(1)} all-to-all(bf16[32,4,1024]{2,1,0:T(4,128)(2,1)S(1)} %get-tuple-element.10), channel_id=1, replica_groups=mesh['tm'=8,'space'=4] {'tm','space'}, dimensions={0} | all-to-all | bytes 524288 | tf_op jit(solution)/shard_map/all_to_all | solution.py:333
  33.6 6.9 %drift.4 = bf16[32,4,1024]{2,1,0:T(4,128)(2,1)S(1)} custom-call(f32[4,4,128]{2,1,0:T(4,128)S(1)} %get-tuple-element.19.sent_one, f32[4,4,128]{2,1,0:T(4,128)S(1)} %get-tuple-element.18.sent_two, f32[4,4,128]{2,1,0:T(4,128)S(1)} %collective-permute-done.got_one, f32[4,4,128]{2,1,0:T(4,128)S(1)} %collective-permute-done.1.got_two, ...), custom_call_target="tpu_custom_call" | custom-call | flops 3460300800 | bytes 6291456 | tf_op jit(solution)/shard_map/drift/pallas_call | solution.py:283
  40.5 12.7 %all_to_all.16 = bf16[32,4,1024]{2,1,0:T(4,128)(2,1)S(1)} all-to-all(bf16[32,4,1024]{2,1,0:T(4,128)(2,1)S(1)} %drift.4), channel_id=1, replica_groups=mesh['tm'=8,'space'=4] {'tm','space'}, dimensions={0} | all-to-all | bytes 524288 | tf_op jit(solution)/shard_map/all_to_all | solution.py:333
  53.3 6.8 %drift.5 = bf16[8,2,4,1024]{3,2,1,0:T(4,128)(2,1)S(1)} custom-call(f32[4,4,128]{2,1,0:T(4,128)S(1)} %get-tuple-element.19.sent_one, f32[4,4,128]{2,1,0:T(4,128)S(1)} %get-tuple-element.18.sent_two, f32[4,4,128]{2,1,0:T(4,128)S(1)} %collective-permute-done.got_one, f32[4,4,128]{2,1,0:T(4,128)S(1)} %collective-permute-done.1.got_two, ...), custom_call_target="tpu_custom_call" | custom-call | flops 3460300800 | bytes 6291456 | tf_op jit(solution)/shard_map/drift/pallas_call | solution.py:283
  60.1 7.9 %all_to_all.17.sent_ref = bf16[8,2,4,1024]{3,2,1,0:T(4,128)(2,1)S(1)} all-to-all(bf16[8,2,4,1024]{3,2,1,0:T(4,128)(2,1)S(1)} %drift.5), channel_id=1, replica_groups=mesh['tm'=8,'space'=4] {'tm'}, dimensions={0} | all-to-all | bytes 262144 | tf_op jit(solution)/shard_map/all_to_all | solution.py:335
  68.0 0.7 %finish.1 = (f32[1,4,8,128]{3,2,1,0:T(8,128)}, f32[4,8,128]{2,1,0:T(8,128)}) custom-call(f32[4,4,128]{2,1,0:T(4,128)S(1)} %get-tuple-element.19.sent_one, f32[4,4,128]{2,1,0:T(4,128)S(1)} %get-tuple-element.18.sent_two, bf16[8,2,4,1024]{3,2,1,0:T(4,128)(2,1)S(1)} %all_to_all.17.sent_ref, f32[19,8,128]{2,1,0:T(8,128)S(1)} %get-tuple-element.15.refs_5_.factors), custom_call_target="tpu_custom_call" | custom-call | tf_op jit(solution)/shard_map/finish/pallas_call | solution.py:336
Async XLA Ops:
  1.4 7.2 %collective-permute-start.1 = (f32[4,4,128]{2,1,0:T(4,128)S(1)}, f32[4,4,128]{2,1,0:T(4,128)S(1)}, u32[]{:S(2)}, u32[]{:S(2)}) collective-permute-start(f32[4,4,128]{2,1,0:T(4,128)S(1)} %get-tuple-element.18.sent_two), channel_id=1, source_target_pairs={{1,2},{2,1},{5,6},{6,5},{9,10},{10,9},{13,14},{14,13},{17,18},{18,... | collective-permute-start | bytes 24584 | tf_op jit(solution)/shard_map/ppermute | solution.py:317
  2.1 7.5 %collective-permute-start = (f32[4,4,128]{2,1,0:T(4,128)S(1)}, f32[4,4,128]{2,1,0:T(4,128)S(1)}, u32[]{:S(2)}, u32[]{:S(2)}) collective-permute-start(f32[4,4,128]{2,1,0:T(4,128)S(1)} %get-tuple-element.19.sent_one), channel_id=1, source_target_pairs={{0,1},{1,0},{2,3},{3,2},{4,5},{5,4},{6,7},{7,6},{8,9},{9,8},{10,11... | collective-permute-start | bytes 24584 | tf_op jit(solution)/shard_map/ppermute | solution.py:317

commit v3 on v2

--- a/solution.py
+++ b/solution.py
@@ -61,16 +61,75 @@
     return [functools.partial(piece, dc) for dc in range(3)]
 
 
+def prep_kernel(slots, owner_ref, steps_hbm, table_hbm, scale_hbm, shift_hbm, wi_hbm, wo_hbm, w1_hbm, w2_hbm,
+                scale_ref, shift_ref, wi_ref, wo_ref, factors, u1, u2, steps_ref, table_ref, w1, w2, block, tail,
+                wi_in, wo_in, wi_rows, wo_rows, sems):
+    loads = [pltpu.make_async_copy(src, dst, sems.at[n]) for n, (src, dst) in enumerate(
+        ((steps_hbm, steps_ref), (w1_hbm, w1), (wi_hbm, wi_in), (wo_hbm, wo_in), (w2_hbm, w2), (table_hbm, table_ref)))]
+    for load in loads:
+        load.start()
+    blocks = scale_hbm.shape[1] // COLS
+    loads[0].wait()
+    t_step = steps_ref[lax.axis_index("tm")]
+    begin = pl.multiple_of(jnp.minimum(t_step // COLS, blocks - 1) * COLS, COLS)
+    columns = []
+    for n, src in enumerate((scale_hbm, shift_hbm)):
+        columns.append(pltpu.make_async_copy(src.at[:, pl.ds(begin, COLS)], block.at[n], sems.at[6 + 2 * n]))
+        columns.append(pltpu.make_async_copy(src.at[:, blocks * COLS:], tail.at[n], sems.at[7 + 2 * n]))
+    for load in columns:
+        load.start()
+    chan, lat = w1.shape[1], wi_in.shape[1]
+    slot = lax.axis_index("tm")
+    wi_rows[...] = jnp.zeros_like(wi_rows)
+    wo_rows[...] = jnp.zeros_like(wo_rows)
+    for load in loads[1:4]:
+        load.wait()
+    for t in range(9):
+        wi_rows[t * lat:(t + 1) * lat, :chan] = wi_in[t].astype(F32)
+        wo_rows[t * TAP_ROWS:t * TAP_ROWS + lat] = wo_in[t].astype(F32)
+    wi_ref[...] = jnp.transpose(wi_rows[...])[:chan].astype(BF)
+    wo_ref[...] = wo_rows[...].astype(BF)
+    for work in weight_pieces(w1, u1):
+        work()
+    for load in loads[4:] + columns:
+        load.wait()
+    for work in weight_pieces(w2, u2):
+        work()
+    write_factors(factors, owner_ref, steps_ref, table_ref, slot, slots)
+    for n, (dst, add) in enumerate(((scale_ref, 1.0), (shift_ref, 0.0))):
+        column = None
+        for ref, first in ((block, begin), (tail, blocks * COLS)):
+            chosen = lax.broadcasted_iota(jnp.int32, ref.shape[1:], 1) + first == t_step
+            part = jnp.sum(jnp.where(chosen, ref[n], 0.0), axis=1, keepdims=True)
+            column = part if column is None else column + part
+        dst[...] = jnp.broadcast_to(0.5 * (column + add), dst.shape)
+
+
+def prep_call(slots, chan, scalars, given):
+    V = pltpu.VMEM
+    padded = (chan + COLS - 1) // COLS * COLS
+    stay = lambda a: pltpu.with_memory_space_constraint(a, pltpu.HBM)
+    scale, shift, wi, wo, w1, w2 = given
+    return pl.pallas_call(
+        functools.partial(prep_kernel, slots),
+        out_shape=[V((chan, COLS), F32), V((chan, COLS), F32), V((chan, COLS), BF), V((9 * TAP_ROWS, chan), BF),
+                   V((2 * slots + 3, 8, COLS), F32), V((4, chan, 3 * chan), BF), V((4, chan, 3 * chan), BF)],
+        in_specs=[SMEM_SPEC] + [pl.BlockSpec(memory_space=pltpu.HBM)] * 8,
+        out_specs=[VMEM_SPEC] * 7,
+        scratch_shapes=[pltpu.SMEM(scalars[1].shape, jnp.int32), pltpu.SMEM(scalars[2].shape, F32), V(w1.shape, BF),
+                        V(w2.shape, BF), V((2, chan, COLS), F32), V((2, chan, scale.shape[1] % COLS), F32), V(wi.shape, BF),
+                        V(wo.shape, BF), V((COLS, padded), F32), V((9 * TAP_ROWS, chan), F32),
+                        pltpu.SemaphoreType.DMA((10,))],
+        compiler_params=pltpu.CompilerParams(vmem_limit_bytes=16 << 20),
+        cost_estimate=pl.CostEstimate(flops=1 << 20, transcendentals=0, bytes_accessed=8 << 20),
+        name="prep",
+    )(scalars[0], *(stay(a) for a in scalars[1:]), *(stay(a) for a in given))
+
+
 def drift_kernel(first, last, copies, slots, spaces, rows, sent_one, sent_two, got_one, got_two, *refs):
-    if first:
-        (owner_ref, steps_ref, table_ref, scale_hbm, shift_hbm, wi_hbm, wo_hbm, w1_hbm, w2_hbm, out_ref, *kept) = refs[:17]
-        (w1, w2, scale_all, shift_all, wi_in, wo_in, wi_rows, wo_rows, sems, *refs) = refs[17:]
-        loads = [pltpu.make_async_copy(src, dst, sems.at[n]) for n, (src, dst) in enumerate(
-            ((wi_hbm, wi_in), (wo_hbm, wo_in), (w1_hbm, w1), (scale_hbm, scale_all), (shift_hbm, shift_all), (w2_hbm, w2)))]
-        for load in loads:
-            load.start()
-    else:
-        (sent_ref, *kept, out_ref), refs = refs[:9], refs[9:]
+    if not first:
+        sent_ref, *refs = refs
+    (*kept, out_ref), refs = refs[:8], refs[8:]
     scale_ref, shift_ref, wi_ref, wo_ref, factors, u1, u2 = kept
     state, cols_in, keep, row_a, row_b, act_a, act_b, taps_out, prods = refs
     chan = scale_ref.shape[0]
@@ -84,31 +143,6 @@
             return v
         at = space * rows + row
         return v * jnp.where((at >= 0) & (at < spaces * rows), 1.0, 0.0).astype(F32)
-
-    before_one, beside_one = [], []
-    if first:
-        wi_rows[...] = jnp.zeros_like(wi_rows)
-        wo_rows[...] = jnp.zeros_like(wo_rows)
-        write_factors(factors, owner_ref, steps_ref, table_ref, device_slot, slots)
-        loads[0].wait()
-        loads[1].wait()
-        for t in range(9):
-            wi_rows[t * lat:(t + 1) * lat, :chan] = wi_in[t].astype(F32)
-            wo_rows[t * TAP_ROWS:t * TAP_ROWS + lat] = wo_in[t].astype(F32)
-        wi_ref[...] = jnp.transpose(wi_rows[...])[:chan].astype(BF)
-        wo_ref[...] = wo_rows[...].astype(BF)
-
-        def modulation():
-            t_step = steps_ref[device_slot]
-            loads[3].wait()
-            loads[4].wait()
-            for src, dst, add in ((scale_all, scale_ref, 1.0), (shift_all, shift_ref, 0.0)):
-                chosen = lax.broadcasted_iota(jnp.int32, src.shape, 1) == t_step
-                column = jnp.sum(jnp.where(chosen, src[...], 0.0), axis=1, keepdims=True)
-                dst[...] = jnp.broadcast_to(0.5 * (column + add), dst.shape)
-
-        before_one = [loads[2].wait] + weight_pieces(w1, u1)
-        beside_one = [[modulation], [], [loads[5].wait] + weight_pieces(w2, u2)]
 
     own_rows = start_rows(space, got_two, got_one) + start_rows(space, sent_two, sent_one)
     own_rows += start_rows(space, sent_one, sent_two) + start_rows(space, got_one, got_two)
@@ -206,15 +240,10 @@
         while ready <= pairs[-1] + 1:
             first_layer(ready)
             ready += 1
-        for work in before_one:
-            work()
-        before_one = []
         beside = list(waiting)
         for j in range(ready, min(pairs[-1] + 4, pairs_one + 1)):
             beside.append(functools.partial(first_layer, j))
             ready = j + 1
-        if beside_one:
-            beside += beside_one.pop(0)
         conv(act_a, u1, pairs, beside, slot)
         waiting = [functools.partial(finish_one, 2 * pairs[0] + n, slot, n) for n in range(2 * len(pairs))]
         slot = 1 - slot
@@ -260,20 +289,9 @@
 
 
 def drift_call(first, last, copies, slots, spaces, rows, chan, lat, tensors):
-    V, S = pltpu.VMEM, jax.ShapeDtypeStruct
-    hbm = pl.BlockSpec(memory_space=pltpu.HBM)
-    padded = (chan + COLS - 1) // COLS * COLS
-    outs = [S((copies, 2, lat, rows * COLS) if last else (copies, lat, rows * COLS), BF)]
-    scratch = []
-    specs = [VMEM_SPEC] * 12
-    if first:
-        specs = [VMEM_SPEC] * 4 + [SMEM_SPEC] * 3 + [hbm] * 6
-        outs += [V((chan, COLS), F32), V((chan, COLS), F32), V((chan, COLS), BF), V((9 * TAP_ROWS, chan), BF),
-                 V((2 * slots + 3, 8, COLS), F32), V((4, chan, 3 * chan), BF), V((4, chan, 3 * chan), BF)]
-        scratch = [V((9, chan, chan), BF), V((9, chan, chan), BF), V(tensors[7].shape, F32), V(tensors[8].shape, F32),
-                   V(tensors[9].shape, BF), V(tensors[10].shape, BF), V((COLS, padded), F32),
-                   V((9 * TAP_ROWS, chan), F32), pltpu.SemaphoreType.DMA((6,))]
-    scratch += [
+    V = pltpu.VMEM
+    out = jax.ShapeDtypeStruct((copies, 2, lat, rows * COLS) if last else (copies, lat, rows * COLS), BF)
+    scratch = [
         V((lat, (rows + 8) * COLS), F32), V((48, (rows + 6) * COLS), F32), V((rows + 6, chan, COLS), BF),
         V((rows + 6, chan, COLS), F32), V((rows + 4, chan, COLS), F32), V(((rows + 4) // 2, 4, 3, chan, COLS), BF),
         V(((rows + 2) // 2, 4, 3, chan, COLS), BF), V((rows + 2, 9 * TAP_ROWS, COLS), F32),
@@ -282,11 +300,11 @@
     passes = 2 * chan * (3 * chan) * 2 * COLS * (rows + 4 + rows + 2)
     return pl.pallas_call(
         functools.partial(drift_kernel, first, last, copies, slots, spaces, rows),
-        out_shape=outs,
-        in_specs=specs,
-        out_specs=[VMEM_SPEC] * len(outs),
+        out_shape=out,
+        in_specs=[VMEM_SPEC] * len(tensors),
+        out_specs=VMEM_SPEC,
         scratch_shapes=scratch,
-        compiler_params=pltpu.CompilerParams(vmem_limit_bytes=(32 if first else 25) << 20),
+        compiler_params=pltpu.CompilerParams(vmem_limit_bytes=25 << 20),
         cost_estimate=pl.CostEstimate(flops=passes, transcendentals=36 * chan * COLS, bytes_accessed=6 << 20),
         name="drift",
     )(*tensors)
@@ -324,14 +342,13 @@
     state = neighbour_rows(latents[0])
     call = functools.partial(drift_call, slots=slots, spaces=spaces, rows=rows, chan=w_one.shape[1], lat=lat)
     everyone = slots * spaces
-    stay = lambda a: pltpu.with_memory_space_constraint(a, pltpu.HBM)
-    given = (mod_scale.T, mod_shift.T, jnp.transpose(w_in, (0, 2, 1)), w_out, w_one, w_two)
-    drift, *weights = call(True, False, everyone, tensors=(
-        *state, owner_slot, stay(slot_steps), stay(step_table), *(stay(a) for a in given)))
+    weights = prep_call(slots, w_one.shape[1], (owner_slot, slot_steps, step_table), (
+        mod_scale.T, mod_shift.T, jnp.transpose(w_in, (0, 2, 1)), w_out, w_one, w_two))
+    drift = call(True, False, everyone, tensors=(*state, *weights))
     for picard_step in range(1, ITERS):
         last = picard_step == ITERS - 1
         sent = lax.all_to_all(drift, ("tm", "space"), 0, 0).reshape(slots, spaces, lat, rows * COLS)
-        drift, = call(False, last, slots if last else everyone, tensors=(*state, sent, *weights))
+        drift = call(False, last, slots if last else everyone, tensors=(*state, sent, *weights))
     sent = lax.all_to_all(drift, "tm", 0, 0)
     return pl.pallas_call(
         functools.partial(finish_kernel, slots),

time: 69.2 us -> 67.6 us (0.977)
  waiting for transfers between devices: 0.97 us -> 0.01 us
    pallas_call x0 -> x1, Pallas kernels: none -> 3.94 us  [prep_call(): pl.pallas_call(functools.partial(prep_kernel, slots), out_shape=[V((chan,...]
    pallas_call x3, Pallas kernels: 23.4 us -> 19.5 us  [drift_call(): pl.pallas_call(functools.partial(drift_kernel, first, last, copies, slots...]
    ppermute x1, waiting for transfers between devices: 0.97 us -> 0.01 us  [neighbour_rows(): lax.ppermute(one, 'space', swap(0))]
  transfers between devices with their start and end apart: 2 -> 2, of which waited for: 1 -> 0; matrix products, arithmetic and copies ran while one was open for 0% -> 0% of each run, Pallas kernels for 0% -> 6%
where the time goes in v3:
time: 67.6 us; the launch traced here: 67.2 us
  blocking collectives  34.3 us (51%)
  Pallas kernels  24.2 us (36%)
  starting transfers between devices  6.56 us (10%)
  between operations  1.35 us (2%)
  other arithmetic  0.8 us (1%)
    all_to_all x2, blocking collectives, body(): lax.all_to_all(drift, ('tm', 'space'), 0, 0)  26.3 us
    pallas_call x3, Pallas kernels, drift_call(): pl.pallas_call(functools.partial(drift_kernel, first, last, copies, slots...  19.5 us
    all_to_all x1, blocking collectives, body(): sent = lax.all_to_all(drift, 'tm', 0, 0)  7.92 us
    ppermute x1, starting transfers between devices, neighbour_rows(): lax.ppermute(one, 'space', swap(0))  5.91 us
    pallas_call x1, Pallas kernels, prep_call(): pl.pallas_call(functools.partial(prep_kernel, slots), out_shape=[V((chan,...  3.94 us
  transfers between devices with their start and end apart: 2, of which 0 were waited for; matrix products, arithmetic and copies ran while one was open for 0% of the time, Pallas kernels for 6%

profile of v3, /device:TPU:0, one launch (start us, length us, event | category | flops | bytes accessed | tf_op | source)
XLA Modules:
  0.0 67.2 jit_solution(6508474974110838385)
XLA Ops:
  0.6 0.8 %slice_select_fusion = (f32[4,4,128]{2,1,0:T(4,128)S(1)}, f32[4,4,128]{2,1,0:T(4,128)S(1)}) fusion(f32[4,8,128]{2,1,0:T(8,128)} %bitcast.11, pred[]{:T(512)S(6)} %eq.5), kind=kLoop, calls=%fused_computation | loop fusion | flops 4096 | bytes 32769 | tf_op jit(solution)/shard_map/jit(_where)/select_n | solution.py:334
  1.4 0.6 collective-permute-start.1
  2.1 5.9 %collective-permute-start = (f32[4,4,128]{2,1,0:T(4,128)S(1)}, f32[4,4,128]{2,1,0:T(4,128)S(1)}, u32[]{:S(2)}, u32[]{:S(2)}) collective-permute-start(f32[4,4,128]{2,1,0:T(4,128)S(1)} %get-tuple-element.17.sent_one), channel_id=1, source_target_pairs={{0,1},{1,0},{2,3},{3,2},{4,5},{5,4},{6,7},{7,6},{8,9},{9,8},{10,11... | collective-permute-start | bytes 24584 | tf_op jit(solution)/shard_map/ppermute | solution.py:335
  8.7 3.9 %prep.1 = (f32[320,128]{1,0:T(8,128)S(1)}, f32[320,128]{1,0:T(8,128)S(1)}, bf16[320,128]{1,0:T(8,128)(2,1)S(1)}, bf16[72,320]{1,0:T(8,128)(2,1)S(1)}, f32[19,8,1...) custom-call(s32[1]{0:T(128)S(6)} %copy.12.owner_ref, s32[8]{0:T(128)} %steps_hbm.1, ...), custom_call_target="tpu_custom_call" | custom-call | flops 1048576 | bytes 8388608 | tf_op jit(solution)/shard_map/prep/pallas_call | solution.py:113
  12.6 0.0 collective-permute-done.1.got_two
  12.6 0.0 collective-permute-done.got_one
  12.6 6.5 %drift.3 = bf16[32,4,1024]{2,1,0:T(4,128)(2,1)S(1)} custom-call(f32[4,4,128]{2,1,0:T(4,128)S(1)} %get-tuple-element.17.sent_one, f32[4,4,128]{2,1,0:T(4,128)S(1)} %get-tuple-element.16.sent_two, f32[4,4,128]{2,1,0:T(4,128)S(1)} %collective-permute-done.got_one, f32[4,4,128]{2,1,0:T(4,128)S(1)} %collective-permute-done.1.got_two, ...), custom_call_target="tpu_custom_call" | custom-call | flops 3460300800 | bytes 6291456 | tf_op jit(solution)/shard_map/drift/pallas_call | solution.py:301
  19.1 13.6 %all_to_all.15 = bf16[32,4,1024]{2,1,0:T(4,128)(2,1)S(1)} all-to-all(bf16[32,4,1024]{2,1,0:T(4,128)(2,1)S(1)} %drift.3), channel_id=1, replica_groups=mesh['tm'=8,'space'=4] {'tm','space'}, dimensions={0} | all-to-all | bytes 524288 | tf_op jit(solution)/shard_map/all_to_all | solution.py:350
  32.7 6.5 %drift.4 = bf16[32,4,1024]{2,1,0:T(4,128)(2,1)S(1)} custom-call(f32[4,4,128]{2,1,0:T(4,128)S(1)} %get-tuple-element.17.sent_one, f32[4,4,128]{2,1,0:T(4,128)S(1)} %get-tuple-element.16.sent_two, f32[4,4,128]{2,1,0:T(4,128)S(1)} %collective-permute-done.got_one, f32[4,4,128]{2,1,0:T(4,128)S(1)} %collective-permute-done.1.got_two, ...), custom_call_target="tpu_custom_call" | custom-call | flops 3460300800 | bytes 6291456 | tf_op jit(solution)/shard_map/drift/pallas_call | solution.py:301
  39.3 12.7 %all_to_all.16 = bf16[32,4,1024]{2,1,0:T(4,128)(2,1)S(1)} all-to-all(bf16[32,4,1024]{2,1,0:T(4,128)(2,1)S(1)} %drift.4), channel_id=1, replica_groups=mesh['tm'=8,'space'=4] {'tm','space'}, dimensions={0} | all-to-all | bytes 524288 | tf_op jit(solution)/shard_map/all_to_all | solution.py:350
  52.0 6.5 %drift.5 = bf16[8,2,4,1024]{3,2,1,0:T(4,128)(2,1)S(1)} custom-call(f32[4,4,128]{2,1,0:T(4,128)S(1)} %get-tuple-element.17.sent_one, f32[4,4,128]{2,1,0:T(4,128)S(1)} %get-tuple-element.16.sent_two, f32[4,4,128]{2,1,0:T(4,128)S(1)} %collective-permute-done.got_one, f32[4,4,128]{2,1,0:T(4,128)S(1)} %collective-permute-done.1.got_two, ...), custom_call_target="tpu_custom_call" | custom-call | flops 3460300800 | bytes 6291456 | tf_op jit(solution)/shard_map/drift/pallas_call | solution.py:301
  58.5 7.9 %all_to_all.17.sent_ref = bf16[8,2,4,1024]{3,2,1,0:T(4,128)(2,1)S(1)} all-to-all(bf16[8,2,4,1024]{3,2,1,0:T(4,128)(2,1)S(1)} %drift.5), channel_id=1, replica_groups=mesh['tm'=8,'space'=4] {'tm'}, dimensions={0} | all-to-all | bytes 262144 | tf_op jit(solution)/shard_map/all_to_all | solution.py:352
  66.4 0.7 %finish.1 = (f32[1,4,8,128]{3,2,1,0:T(8,128)}, f32[4,8,128]{2,1,0:T(8,128)}) custom-call(f32[4,4,128]{2,1,0:T(4,128)S(1)} %get-tuple-element.17.sent_one, f32[4,4,128]{2,1,0:T(4,128)S(1)} %get-tuple-element.16.sent_two, bf16[8,2,4,1024]{3,2,1,0:T(4,128)(2,1)S(1)} %all_to_all.17.sent_ref, f32[19,8,128]{2,1,0:T(8,128)S(1)} %get-tuple-element.13.refs_4_.refs_5_.factors), custom_call_target="tpu_custom_call" | custom-call | tf_op jit(solution)/shard_map/finish/pallas_call | solution.py:353
Async XLA Ops:
  1.4 11.2 %collective-permute-start.1 = (f32[4,4,128]{2,1,0:T(4,128)S(1)}, f32[4,4,128]{2,1,0:T(4,128)S(1)}, u32[]{:S(2)}, u32[]{:S(2)}) collective-permute-start(f32[4,4,128]{2,1,0:T(4,128)S(1)} %get-tuple-element.16.sent_two), channel_id=1, source_target_pairs={{1,2},{2,1},{5,6},{6,5},{9,10},{10,9},{13,14},{14,13},{17,18},{18,... | collective-permute-start | bytes 24584 | tf_op jit(solution)/shard_map/ppermute | solution.py:335
  2.1 10.5 %collective-permute-start = (f32[4,4,128]{2,1,0:T(4,128)S(1)}, f32[4,4,128]{2,1,0:T(4,128)S(1)}, u32[]{:S(2)}, u32[]{:S(2)}) collective-permute-start(f32[4,4,128]{2,1,0:T(4,128)S(1)} %get-tuple-element.17.sent_one), channel_id=1, source_target_pairs={{0,1},{1,0},{2,3},{3,2},{4,5},{5,4},{6,7},{7,6},{8,9},{9,8},{10,11... | collective-permute-start | bytes 24584 | tf_op jit(solution)/shard_map/ppermute | solution.py:335

commit v4 on v3

--- a/solution.py
+++ b/solution.py
@@ -65,8 +65,10 @@
                 scale_ref, shift_ref, wi_ref, wo_ref, factors, u1, u2, steps_ref, table_ref, w1, w2, block, tail,
                 wi_in, wo_in, wi_rows, wo_rows, sems):
     loads = [pltpu.make_async_copy(src, dst, sems.at[n]) for n, (src, dst) in enumerate(
-        ((steps_hbm, steps_ref), (w1_hbm, w1), (wi_hbm, wi_in), (wo_hbm, wo_in), (w2_hbm, w2), (table_hbm, table_ref)))]
-    for load in loads:
+        ((steps_hbm, steps_ref), (wi_hbm, wi_in), (wo_hbm, wo_in), (table_hbm, table_ref)))]
+    taps = {(n, dc): [pltpu.make_async_copy(src.at[3 * dr + dc], dst.at[3 * dr + dc], sems.at[10 + 9 * n + 3 * dc + dr])
+                      for dr in range(3)] for n, (src, dst) in enumerate(((w1_hbm, w1), (w2_hbm, w2))) for dc in range(3)}
+    for load in loads + sum(taps.values(), []):
         load.start()
     blocks = scale_hbm.shape[1] // COLS
     loads[0].wait()
@@ -74,27 +76,28 @@
     begin = pl.multiple_of(jnp.minimum(t_step // COLS, blocks - 1) * COLS, COLS)
     columns = []
     for n, src in enumerate((scale_hbm, shift_hbm)):
-        columns.append(pltpu.make_async_copy(src.at[:, pl.ds(begin, COLS)], block.at[n], sems.at[6 + 2 * n]))
-        columns.append(pltpu.make_async_copy(src.at[:, blocks * COLS:], tail.at[n], sems.at[7 + 2 * n]))
+        columns.append(pltpu.make_async_copy(src.at[:, pl.ds(begin, COLS)], block.at[n], sems.at[4 + 2 * n]))
+        columns.append(pltpu.make_async_copy(src.at[:, blocks * COLS:], tail.at[n], sems.at[5 + 2 * n]))
     for load in columns:
         load.start()
     chan, lat = w1.shape[1], wi_in.shape[1]
     slot = lax.axis_index("tm")
     wi_rows[...] = jnp.zeros_like(wi_rows)
     wo_rows[...] = jnp.zeros_like(wo_rows)
-    for load in loads[1:4]:
+    for load in loads[1:3]:
         load.wait()
     for t in range(9):
         wi_rows[t * lat:(t + 1) * lat, :chan] = wi_in[t].astype(F32)
         wo_rows[t * TAP_ROWS:t * TAP_ROWS + lat] = wo_in[t].astype(F32)
     wi_ref[...] = jnp.transpose(wi_rows[...])[:chan].astype(BF)
     wo_ref[...] = wo_rows[...].astype(BF)
-    for work in weight_pieces(w1, u1):
-        work()
-    for load in loads[4:] + columns:
+    for n, (w, u) in enumerate(((w1, u1), (w2, u2))):
+        for dc, work in enumerate(weight_pieces(w, u)):
+            for load in taps[n, dc]:
+                load.wait()
+            work()
+    for load in loads[3:] + columns:
         load.wait()
-    for work in weight_pieces(w2, u2):
-        work()
     write_factors(factors, owner_ref, steps_ref, table_ref, slot, slots)
     for n, (dst, add) in enumerate(((scale_ref, 1.0), (shift_ref, 0.0))):
         column = None
@@ -119,7 +122,7 @@
         scratch_shapes=[pltpu.SMEM(scalars[1].shape, jnp.int32), pltpu.SMEM(scalars[2].shape, F32), V(w1.shape, BF),
                         V(w2.shape, BF), V((2, chan, COLS), F32), V((2, chan, scale.shape[1] % COLS), F32), V(wi.shape, BF),
                         V(wo.shape, BF), V((COLS, padded), F32), V((9 * TAP_ROWS, chan), F32),
-                        pltpu.SemaphoreType.DMA((10,))],
+                        pltpu.SemaphoreType.DMA((28,))],
         compiler_params=pltpu.CompilerParams(vmem_limit_bytes=16 << 20),
         cost_estimate=pl.CostEstimate(flops=1 << 20, transcendentals=0, bytes_accessed=8 << 20),
         name="prep",
@@ -225,11 +228,15 @@
         if row >= 3 and row % 2:
             transformed(row_b, act_b, (row - 3) // 2)
 
+    acts = {}
+
     def finish_two(row, slot, n):
         y = untransformed(slot, n)
         second = (keep[row + 2].astype(F32) + y).astype(BF).astype(F32)
-        act = masked(silu(0.5 * second), row - 1).astype(BF)
-        taps_out[row] = jnp.dot(wo_ref[...], act, preferred_element_type=F32)
+        acts[row] = masked(silu(0.5 * second), row - 1).astype(BF)
+        if row % 2:
+            both = jnp.concatenate([acts.pop(row - 1), acts.pop(row)], axis=1)
+            taps_out[row // 2] = jnp.dot(wo_ref[...], both, preferred_element_type=F32)
 
     pairs_one, pairs_two = (rows + 4) // 2, (rows + 2) // 2
     steps_one = [tuple(range(p, min(p + 2, pairs_one))) for p in range(0, pairs_one, 2)]
@@ -267,7 +274,8 @@
             v = None
             for dr in range(3):
                 t = 3 * dr + dc
-                p = taps_out[r + dr, TAP_ROWS * t:TAP_ROWS * (t + 1)]
+                q = r + dr
+                p = taps_out[q // 2, TAP_ROWS * t:TAP_ROWS * (t + 1), q % 2 * COLS:(q % 2 + 1) * COLS]
                 v = p if v is None else v + p
             if dc == 0:
                 v = jnp.where(lane8 == 0, 0.0, pltpu.roll(v, 1, 1))
@@ -294,7 +302,7 @@
     scratch = [
         V((lat, (rows + 8) * COLS), F32), V((48, (rows + 6) * COLS), F32), V((rows + 6, chan, COLS), BF),
         V((rows + 6, chan, COLS), F32), V((rows + 4, chan, COLS), F32), V(((rows + 4) // 2, 4, 3, chan, COLS), BF),
-        V(((rows + 2) // 2, 4, 3, chan, COLS), BF), V((rows + 2, 9 * TAP_ROWS, COLS), F32),
+        V(((rows + 2) // 2, 4, 3, chan, COLS), BF), V(((rows + 2) // 2, 9 * TAP_ROWS, 2 * COLS), F32),
         V((2, 4, chan, 2 * COLS), F32),
     ]
     passes = 2 * chan * (3 * chan) * 2 * COLS * (rows + 4 + rows + 2)

time: 67.6 us -> 66.3 us (0.981)
  Pallas kernels: 24.2 us -> 22.9 us
    pallas_call x3, Pallas kernels: 19.5 us -> 18.6 us  [drift_call(): pl.pallas_call(functools.partial(drift_kernel, first, last, copies, slots...]
  transfers between devices with their start and end apart: 2 -> 2, of which waited for: 0 -> 0; matrix products, arithmetic and copies ran while one was open for 0% -> 0% of each run, Pallas kernels for 6% -> 5%
where the time goes in v4:
time: 66.3 us; the launch traced here: 65.8 us
  blocking collectives  34.2 us (52%)
  Pallas kernels  22.9 us (35%)
  starting transfers between devices  6.56 us (10%)
  between operations  1.35 us (2%)
  other arithmetic  0.8 us (1%)
    all_to_all x2, blocking collectives, body(): lax.all_to_all(drift, ('tm', 'space'), 0, 0)  26.3 us
    pallas_call x3, Pallas kernels, drift_call(): pl.pallas_call(functools.partial(drift_kernel, first, last, copies, slots...  18.6 us
    all_to_all x1, blocking collectives, body(): sent = lax.all_to_all(drift, 'tm', 0, 0)  7.92 us
    ppermute x1, starting transfers between devices, neighbour_rows(): lax.ppermute(one, 'space', swap(0))  5.91 us
    pallas_call x1, Pallas kernels, prep_call(): pl.pallas_call(functools.partial(prep_kernel, slots), out_shape=[V((chan,...  3.53 us
  transfers between devices with their start and end apart: 2, of which 0 were waited for; matrix products, arithmetic and copies ran while one was open for 0% of the time, Pallas kernels for 5%

profile of v4, /device:TPU:0, one launch (start us, length us, event | category | flops | bytes accessed | tf_op | source)
XLA Modules:
  0.0 65.8 jit_solution(6451278757216528220)
XLA Ops:
  0.6 0.8 %slice_select_fusion = (f32[4,4,128]{2,1,0:T(4,128)S(1)}, f32[4,4,128]{2,1,0:T(4,128)S(1)}) fusion(f32[4,8,128]{2,1,0:T(8,128)} %bitcast.11, pred[]{:T(512)S(6)} %eq.5), kind=kLoop, calls=%fused_computation | loop fusion | flops 4096 | bytes 32769 | tf_op jit(solution)/shard_map/jit(_where)/select_n | solution.py:342
  1.4 0.6 collective-permute-start.1
  2.1 5.9 %collective-permute-start = (f32[4,4,128]{2,1,0:T(4,128)S(1)}, f32[4,4,128]{2,1,0:T(4,128)S(1)}, u32[]{:S(2)}, u32[]{:S(2)}) collective-permute-start(f32[4,4,128]{2,1,0:T(4,128)S(1)} %get-tuple-element.17.sent_one), channel_id=1, source_target_pairs={{0,1},{1,0},{2,3},{3,2},{4,5},{5,4},{6,7},{7,6},{8,9},{9,8},{10,11... | collective-permute-start | bytes 24584 | tf_op jit(solution)/shard_map/ppermute | solution.py:343
  8.7 3.5 %prep.1 = (f32[320,128]{1,0:T(8,128)S(1)}, f32[320,128]{1,0:T(8,128)S(1)}, bf16[320,128]{1,0:T(8,128)(2,1)S(1)}, bf16[72,320]{1,0:T(8,128)(2,1)S(1)}, f32[19,8,1...) custom-call(s32[1]{0:T(128)S(6)} %copy.12.owner_ref, s32[8]{0:T(128)} %steps_hbm.1, ...), custom_call_target="tpu_custom_call" | custom-call | flops 1048576 | bytes 8388608 | tf_op jit(solution)/shard_map/prep/pallas_call | solution.py:116
  12.2 0.0 collective-permute-done.1.got_two
  12.2 0.0 collective-permute-done.got_one
  12.2 6.2 %drift.3 = bf16[32,4,1024]{2,1,0:T(4,128)(2,1)S(1)} custom-call(f32[4,4,128]{2,1,0:T(4,128)S(1)} %get-tuple-element.17.sent_one, f32[4,4,128]{2,1,0:T(4,128)S(1)} %get-tuple-element.16.sent_two, f32[4,4,128]{2,1,0:T(4,128)S(1)} %collective-permute-done.got_one, f32[4,4,128]{2,1,0:T(4,128)S(1)} %collective-permute-done.1.got_two, ...), custom_call_target="tpu_custom_call" | custom-call | flops 3460300800 | bytes 6291456 | tf_op jit(solution)/shard_map/drift/pallas_call | solution.py:309
  18.5 13.6 %all_to_all.15 = bf16[32,4,1024]{2,1,0:T(4,128)(2,1)S(1)} all-to-all(bf16[32,4,1024]{2,1,0:T(4,128)(2,1)S(1)} %drift.3), channel_id=1, replica_groups=mesh['tm'=8,'space'=4] {'tm','space'}, dimensions={0} | all-to-all | bytes 524288 | tf_op jit(solution)/shard_map/all_to_all | solution.py:358
  32.1 6.2 %drift.4 = bf16[32,4,1024]{2,1,0:T(4,128)(2,1)S(1)} custom-call(f32[4,4,128]{2,1,0:T(4,128)S(1)} %get-tuple-element.17.sent_one, f32[4,4,128]{2,1,0:T(4,128)S(1)} %get-tuple-element.16.sent_two, f32[4,4,128]{2,1,0:T(4,128)S(1)} %collective-permute-done.got_one, f32[4,4,128]{2,1,0:T(4,128)S(1)} %collective-permute-done.1.got_two, ...), custom_call_target="tpu_custom_call" | custom-call | flops 3460300800 | bytes 6291456 | tf_op jit(solution)/shard_map/drift/pallas_call | solution.py:309
  38.3 12.7 %all_to_all.16 = bf16[32,4,1024]{2,1,0:T(4,128)(2,1)S(1)} all-to-all(bf16[32,4,1024]{2,1,0:T(4,128)(2,1)S(1)} %drift.4), channel_id=1, replica_groups=mesh['tm'=8,'space'=4] {'tm','space'}, dimensions={0} | all-to-all | bytes 524288 | tf_op jit(solution)/shard_map/all_to_all | solution.py:358
  51.0 6.2 %drift.5 = bf16[8,2,4,1024]{3,2,1,0:T(4,128)(2,1)S(1)} custom-call(f32[4,4,128]{2,1,0:T(4,128)S(1)} %get-tuple-element.17.sent_one, f32[4,4,128]{2,1,0:T(4,128)S(1)} %get-tuple-element.16.sent_two, f32[4,4,128]{2,1,0:T(4,128)S(1)} %collective-permute-done.got_one, f32[4,4,128]{2,1,0:T(4,128)S(1)} %collective-permute-done.1.got_two, ...), custom_call_target="tpu_custom_call" | custom-call | flops 3460300800 | bytes 6291456 | tf_op jit(solution)/shard_map/drift/pallas_call | solution.py:309
  57.2 7.9 %all_to_all.17.sent_ref = bf16[8,2,4,1024]{3,2,1,0:T(4,128)(2,1)S(1)} all-to-all(bf16[8,2,4,1024]{3,2,1,0:T(4,128)(2,1)S(1)} %drift.5), channel_id=1, replica_groups=mesh['tm'=8,'space'=4] {'tm'}, dimensions={0} | all-to-all | bytes 262144 | tf_op jit(solution)/shard_map/all_to_all | solution.py:360
  65.1 0.7 %finish.1 = (f32[1,4,8,128]{3,2,1,0:T(8,128)}, f32[4,8,128]{2,1,0:T(8,128)}) custom-call(f32[4,4,128]{2,1,0:T(4,128)S(1)} %get-tuple-element.17.sent_one, f32[4,4,128]{2,1,0:T(4,128)S(1)} %get-tuple-element.16.sent_two, bf16[8,2,4,1024]{3,2,1,0:T(4,128)(2,1)S(1)} %all_to_all.17.sent_ref, f32[19,8,128]{2,1,0:T(8,128)S(1)} %get-tuple-element.13.refs_4_.refs_5_.factors), custom_call_target="tpu_custom_call" | custom-call | tf_op jit(solution)/shard_map/finish/pallas_call | solution.py:361
Async XLA Ops:
  1.4 10.8 %collective-permute-start.1 = (f32[4,4,128]{2,1,0:T(4,128)S(1)}, f32[4,4,128]{2,1,0:T(4,128)S(1)}, u32[]{:S(2)}, u32[]{:S(2)}) collective-permute-start(f32[4,4,128]{2,1,0:T(4,128)S(1)} %get-tuple-element.16.sent_two), channel_id=1, source_target_pairs={{1,2},{2,1},{5,6},{6,5},{9,10},{10,9},{13,14},{14,13},{17,18},{18,... | collective-permute-start | bytes 24584 | tf_op jit(solution)/shard_map/ppermute | solution.py:343
  2.1 10.1 %collective-permute-start = (f32[4,4,128]{2,1,0:T(4,128)S(1)}, f32[4,4,128]{2,1,0:T(4,128)S(1)}, u32[]{:S(2)}, u32[]{:S(2)}) collective-permute-start(f32[4,4,128]{2,1,0:T(4,128)S(1)} %get-tuple-element.17.sent_one), channel_id=1, source_target_pairs={{0,1},{1,0},{2,3},{3,2},{4,5},{5,4},{6,7},{7,6},{8,9},{9,8},{10,11... | collective-permute-start | bytes 24584 | tf_op jit(solution)/shard_map/ppermute | solution.py:343

commit v5 on v4

--- a/solution.py
+++ b/solution.py
@@ -131,7 +131,7 @@
 
 def drift_kernel(first, last, copies, slots, spaces, rows, sent_one, sent_two, got_one, got_two, *refs):
     if not first:
-        sent_ref, *refs = refs
+        sent_ref, other_ref, *refs = refs
     (*kept, out_ref), refs = refs[:8], refs[8:]
     scale_ref, shift_ref, wi_ref, wo_ref, factors, u1, u2 = kept
     state, cols_in, keep, row_a, row_b, act_a, act_b, taps_out, prods = refs
@@ -149,21 +149,27 @@
 
     own_rows = start_rows(space, got_two, got_one) + start_rows(space, sent_two, sent_one)
     own_rows += start_rows(space, sent_one, sent_two) + start_rows(space, got_one, got_two)
+    first_core = lax.rem(device_slot, 2) == 0
+
+    def weighed(ref, row):
+        total = None
+        for q in range(slots):
+            term = factors[q, :lat] * ref[q, :, row * COLS:(row + 1) * COLS].astype(F32)
+            total = term if total is None else total + term
+        return total
+
     for k, own in enumerate(own_rows):
         value = own
         if not first:
             row = k - HALO
-            source = space
             if row < 0:
-                source = jnp.maximum(space - 1, 0)
+                total = masked(weighed(sent_ref.at[jnp.maximum(space - 1, 0)], k), row)
             elif row >= rows:
-                source = jnp.minimum(space + 1, spaces - 1)
-            at = slice(row % rows * COLS, (row % rows + 1) * COLS)
-            total = None
-            for q in range(slots):
-                term = factors[q, :lat] * sent_ref[q, source, :, at].astype(F32)
-                total = term if total is None else total + term
-            value = masked(total, row) + factors[2 * slots, :lat] * own
+                total = masked(weighed(sent_ref.at[jnp.minimum(space + 1, spaces - 1)], row - rows), row)
+            else:
+                here, there = weighed(sent_ref.at[space], row % HALO), weighed(other_ref, row % HALO)
+                total = jnp.where(first_core == (row < HALO), here, there)
+            value = total + factors[2 * slots, :lat] * own
         state[:, k * COLS:(k + 1) * COLS] = value.astype(BF).astype(F32)
 
     n_in = rows + 6
@@ -267,6 +273,7 @@
     for work in waiting:
         work()
 
+    highs = []
     lane8 = lax.broadcasted_iota(jnp.int32, (TAP_ROWS, COLS), 1)
     for r in range(rows):
         total = None
@@ -286,19 +293,25 @@
         at = slice(r * COLS, (r + 1) * COLS)
         value = factors[2 * slots + 1, :lat] * drift + factors[2 * slots + 2, :lat] * own_rows[HALO + r]
         high = value.astype(BF)
+        highs.append(high)
         if last:
             low = (value - high.astype(F32)).astype(BF)
-        for n in range(copies):
-            if last:
+            for n in range(copies):
                 out_ref[n, 0, :, at] = high
                 out_ref[n, 1, :, at] = low
-            else:
-                out_ref[n, :, at] = high
+    if not last:
+        for i in range(HALO):
+            at = slice(i * COLS, (i + 1) * COLS)
+            for k in range(spaces):
+                to_first = jnp.where(k <= space, highs[i], highs[HALO + i])
+                to_second = jnp.where(k < space, highs[i], highs[HALO + i])
+                for t in range(slots):
+                    out_ref[k * slots + t, :, at] = to_second if t % 2 else to_first
 
 
 def drift_call(first, last, copies, slots, spaces, rows, chan, lat, tensors):
     V = pltpu.VMEM
-    out = jax.ShapeDtypeStruct((copies, 2, lat, rows * COLS) if last else (copies, lat, rows * COLS), BF)
+    out = jax.ShapeDtypeStruct((copies, 2, lat, rows * COLS) if last else (copies, lat, HALO * COLS), BF)
     scratch = [
         V((lat, (rows + 8) * COLS), F32), V((48, (rows + 6) * COLS), F32), V((rows + 6, chan, COLS), BF),
         V((rows + 6, chan, COLS), F32), V((rows + 4, chan, COLS), F32), V(((rows + 4) // 2, 4, 3, chan, COLS), BF),
@@ -353,10 +366,14 @@
     weights = prep_call(slots, w_one.shape[1], (owner_slot, slot_steps, step_table), (
         mod_scale.T, mod_shift.T, jnp.transpose(w_in, (0, 2, 1)), w_out, w_one, w_two))
     drift = call(True, False, everyone, tensors=(*state, *weights))
+    here = lax.axis_index("space").astype(jnp.uint32)
     for picard_step in range(1, ITERS):
         last = picard_step == ITERS - 1
-        sent = lax.all_to_all(drift, ("tm", "space"), 0, 0).reshape(slots, spaces, lat, rows * COLS)
-        drift = call(False, last, slots if last else everyone, tensors=(*state, sent, *weights))
+        drift, here = lax.optimization_barrier((drift, here))
+        sent = lax.all_to_all(drift, ("space", "tm"), 0, 0).reshape(spaces, slots, lat, HALO * COLS)
+        half = lax.dynamic_index_in_dim(sent, here, 0, keepdims=False)
+        sent = (sent, lax.ppermute(half, "tm", [(t, t ^ 1) for t in range(slots)]))
+        drift = call(False, last, slots if last else everyone, tensors=(*state, *sent, *weights))
     sent = lax.all_to_all(drift, "tm", 0, 0)
     return pl.pallas_call(
         functools.partial(finish_kernel, slots),

time: 66.3 us -> 65.1 us (0.982)
  blocking collectives: 34.2 us -> 29.5 us
  waiting for transfers between devices: 0.01 us -> 1.99 us
  Pallas kernels: 22.9 us -> 23.9 us
    all_to_all x2, blocking collectives: 26.3 us -> 21.6 us  [body(): lax.all_to_all(drift, ('space', 'tm'), 0, 0)]
    ppermute x0 -> x2, waiting for transfers between devices: none -> 1.98 us  [body(): sent = (sent, lax.ppermute(half, 'tm', [(t, t ^ 1) for t in range(slots)]))]
    pallas_call x3, Pallas kernels: 18.6 us -> 19.6 us  [drift_call(): pl.pallas_call(functools.partial(drift_kernel, first, last, copies, slots...]
  transfers between devices with their start and end apart: 2 -> 4, of which waited for: 0 -> 2; matrix products, arithmetic and copies ran while one was open for 0% -> 0% of each run, Pallas kernels for 5% -> 5%
where the time goes in v5:
time: 65.1 us; the launch traced here: 64.7 us
  blocking collectives  29.5 us (45%)
  Pallas kernels  23.9 us (37%)
  starting transfers between devices  7.12 us (11%)
  waiting for transfers between devices  1.99 us (3%)
  between operations  1.36 us (2%)
  other arithmetic  0.8 us (1%)
    all_to_all x2, blocking collectives, body(): lax.all_to_all(drift, ('space', 'tm'), 0, 0)  21.6 us
    pallas_call x3, Pallas kernels, drift_call(): pl.pallas_call(functools.partial(drift_kernel, first, last, copies, slots...  19.6 us
    all_to_all x1, blocking collectives, body(): sent = lax.all_to_all(drift, 'tm', 0, 0)  7.92 us
    ppermute x1, starting transfers between devices, neighbour_rows(): lax.ppermute(one, 'space', swap(0))  5.91 us
    pallas_call x1, Pallas kernels, prep_call(): pl.pallas_call(functools.partial(prep_kernel, slots), out_shape=[V((chan,...  3.53 us
    ppermute x2, waiting for transfers between devices, body(): sent = (sent, lax.ppermute(half, 'tm', [(t, t ^ 1) for t in range(slots)]))  1.98 us
  transfers between devices with their start and end apart: 4, of which 2 were waited for; matrix products, arithmetic and copies ran while one was open for 0% of the time, Pallas kernels for 5%

profile of v5, /device:TPU:0, one launch (start us, length us, event | category | flops | bytes accessed | tf_op | source)
XLA Modules:
  0.0 64.7 jit_solution(13991528399446327538)
XLA Ops:
  0.6 0.8 %slice_select_fusion = (f32[4,4,128]{2,1,0:T(4,128)S(1)}, f32[4,4,128]{2,1,0:T(4,128)S(1)}) fusion(f32[4,8,128]{2,1,0:T(8,128)} %bitcast.17, pred[]{:T(512)S(6)} %eq.5), kind=kLoop, calls=%fused_computation.2 | loop fusion | flops 4096 | bytes 32769 | tf_op jit(solution)/shard_map/jit(_where)/select_n | solution.py:355
  1.4 0.6 %collective-permute-start.1 = (f32[4,4,128]{2,1,0:T(4,128)S(1)}, f32[4,4,128]{2,1,0:T(4,128)S(1)}, u32[]{:S(2)}, u32[]{:S(2)}) collective-permute-start(f32[4,4,128]{2,1,0:T(4,128)S(1)} %get-tuple-element.24.sent_two), channel_id=1, source_target_pairs={{1,2},{2,1},{5,6},{6,5},{9,10},{10,9},{13,14},{14,13},{17,18},{18,... | collective-permute-start | bytes 24584 | tf_op jit(solution)/shard_map/ppermute | solution.py:356
  2.1 5.9 %collective-permute-start = (f32[4,4,128]{2,1,0:T(4,128)S(1)}, f32[4,4,128]{2,1,0:T(4,128)S(1)}, u32[]{:S(2)}, u32[]{:S(2)}) collective-permute-start(f32[4,4,128]{2,1,0:T(4,128)S(1)} %get-tuple-element.25.sent_one), channel_id=1, source_target_pairs={{0,1},{1,0},{2,3},{3,2},{4,5},{5,4},{6,7},{7,6},{8,9},{9,8},{10,11... | collective-permute-start | bytes 24584 | tf_op jit(solution)/shard_map/ppermute | solution.py:356
  8.7 3.5 %prep.1 = (f32[320,128]{1,0:T(8,128)S(1)}, f32[320,128]{1,0:T(8,128)S(1)}, bf16[320,128]{1,0:T(8,128)(2,1)S(1)}, bf16[72,320]{1,0:T(8,128)(2,1)S(1)}, f32[19,8,1...) custom-call(s32[1]{0:T(128)S(6)} %copy.12.owner_ref, s32[8]{0:T(128)} %steps_hbm.1, ...), custom_call_target="tpu_custom_call" | custom-call | flops 1048576 | bytes 8388608 | tf_op jit(solution)/shard_map/prep/pallas_call | solution.py:116
  12.2 0.0 collective-permute-done.1.got_two
  12.2 0.0 collective-permute-done.got_one
  12.2 6.5 %drift.3 = bf16[32,4,512]{2,1,0:T(4,128)(2,1)S(1)} custom-call(f32[4,4,128]{2,1,0:T(4,128)S(1)} %get-tuple-element.25.sent_one, f32[4,4,128]{2,1,0:T(4,128)S(1)} %get-tuple-element.24.sent_two, f32[4,4,128]{2,1,0:T(4,128)S(1)} %collective-permute-done.got_one, f32[4,4,128]{2,1,0:T(4,128)S(1)} %collective-permute-done.1.got_two, ...), custom_call_target="tpu_custom_call" | custom-call | flops 3460300800 | bytes 6291456 | tf_op jit(solution)/shard_map/drift/pallas_call | solution.py:322
  18.8 11.6 %all_to_all.15 = bf16[32,4,512]{2,1,0:T(4,128)(2,1)S(1)} all-to-all(bf16[32,4,512]{2,1,0:T(4,128)(2,1)S(1)} %drift.3), channel_id=1, replica_groups=mesh['tm'=8,'space'=4] {'space','tm'}, dimensions={0} | all-to-all | bytes 262144 | tf_op jit(solution)/shard_map/all_to_all | solution.py:373
  30.4 0.3 collective-permute-start.2
  30.7 1.0 %collective-permute-done.2.refs_1_ = bf16[8,4,512]{2,1,0:T(4,128)(2,1)S(1)} collective-permute-done((bf16[8,4,512]{2,1,0:T(4,128)(2,1)S(1)}, bf16[8,4,512]{2,1,0:T(4,128)(2,1)S(1)}, u32[]{:S(2)}, u32[]{:S(2)}) %collective-permute-start.2) | collective-permute-done | bytes 32800 | tf_op jit(solution)/shard_map/ppermute | solution.py:375
  31.7 6.6 %drift.4 = bf16[32,4,512]{2,1,0:T(4,128)(2,1)S(1)} custom-call(f32[4,4,128]{2,1,0:T(4,128)S(1)} %get-tuple-element.25.sent_one, f32[4,4,128]{2,1,0:T(4,128)S(1)} %get-tuple-element.24.sent_two, f32[4,4,128]{2,1,0:T(4,128)S(1)} %collective-permute-done.got_one, f32[4,4,128]{2,1,0:T(4,128)S(1)} %collective-permute-done.1.got_two, ...), custom_call_target="tpu_custom_call" | custom-call | flops 3460300800 | bytes 6291456 | tf_op jit(solution)/shard_map/drift/pallas_call | solution.py:322
  38.3 10.0 %all_to_all.16 = bf16[32,4,512]{2,1,0:T(4,128)(2,1)S(1)} all-to-all(bf16[32,4,512]{2,1,0:T(4,128)(2,1)S(1)} %drift.4), channel_id=1, replica_groups=mesh['tm'=8,'space'=4] {'space','tm'}, dimensions={0} | all-to-all | bytes 262144 | tf_op jit(solution)/shard_map/all_to_all | solution.py:373
  48.3 0.3 collective-permute-start.3
  48.5 1.0 %collective-permute-done.3.refs_1_ = bf16[8,4,512]{2,1,0:T(4,128)(2,1)S(1)} collective-permute-done((bf16[8,4,512]{2,1,0:T(4,128)(2,1)S(1)}, bf16[8,4,512]{2,1,0:T(4,128)(2,1)S(1)}, u32[]{:S(2)}, u32[]{:S(2)}) %collective-permute-start.3) | collective-permute-done | bytes 32800 | tf_op jit(solution)/shard_map/ppermute | solution.py:375
  49.5 6.5 %drift.5 = bf16[8,2,4,1024]{3,2,1,0:T(4,128)(2,1)S(1)} custom-call(f32[4,4,128]{2,1,0:T(4,128)S(1)} %get-tuple-element.25.sent_one, f32[4,4,128]{2,1,0:T(4,128)S(1)} %get-tuple-element.24.sent_two, f32[4,4,128]{2,1,0:T(4,128)S(1)} %collective-permute-done.got_one, f32[4,4,128]{2,1,0:T(4,128)S(1)} %collective-permute-done.1.got_two, ...), custom_call_target="tpu_custom_call" | custom-call | flops 3460300800 | bytes 6291456 | tf_op jit(solution)/shard_map/drift/pallas_call | solution.py:322
  56.1 7.9 %all_to_all.17.sent_ref = bf16[8,2,4,1024]{3,2,1,0:T(4,128)(2,1)S(1)} all-to-all(bf16[8,2,4,1024]{3,2,1,0:T(4,128)(2,1)S(1)} %drift.5), channel_id=1, replica_groups=mesh['tm'=8,'space'=4] {'tm'}, dimensions={0} | all-to-all | bytes 262144 | tf_op jit(solution)/shard_map/all_to_all | solution.py:377
  64.0 0.7 %finish.1 = (f32[1,4,8,128]{3,2,1,0:T(8,128)}, f32[4,8,128]{2,1,0:T(8,128)}) custom-call(f32[4,4,128]{2,1,0:T(4,128)S(1)} %get-tuple-element.25.sent_one, f32[4,4,128]{2,1,0:T(4,128)S(1)} %get-tuple-element.24.sent_two, bf16[8,2,4,1024]{3,2,1,0:T(4,128)(2,1)S(1)} %all_to_all.17.sent_ref, f32[19,8,128]{2,1,0:T(8,128)S(1)} %get-tuple-element.17.refs_4_.refs_6_.factors), custom_call_target="tpu_custom_call" | custom-call | tf_op jit(solution)/shard_map/finish/pallas_call | solution.py:378
  (2 shorter events, 0.0 us)
Async XLA Ops:
  1.4 10.8 %collective-permute-start.1 = (f32[4,4,128]{2,1,0:T(4,128)S(1)}, f32[4,4,128]{2,1,0:T(4,128)S(1)}, u32[]{:S(2)}, u32[]{:S(2)}) collective-permute-start(f32[4,4,128]{2,1,0:T(4,128)S(1)} %get-tuple-element.24.sent_two), channel_id=1, source_target_pairs={{1,2},{2,1},{5,6},{6,5},{9,10},{10,9},{13,14},{14,13},{17,18},{18,... | collective-permute-start | bytes 24584 | tf_op jit(solution)/shard_map/ppermute | solution.py:356
  2.1 10.1 %collective-permute-start = (f32[4,4,128]{2,1,0:T(4,128)S(1)}, f32[4,4,128]{2,1,0:T(4,128)S(1)}, u32[]{:S(2)}, u32[]{:S(2)}) collective-permute-start(f32[4,4,128]{2,1,0:T(4,128)S(1)} %get-tuple-element.25.sent_one), channel_id=1, source_target_pairs={{0,1},{1,0},{2,3},{3,2},{4,5},{5,4},{6,7},{7,6},{8,9},{9,8},{10,11... | collective-permute-start | bytes 24584 | tf_op jit(solution)/shard_map/ppermute | solution.py:356
  30.4 1.3 %collective-permute-start.2 = (bf16[8,4,512]{2,1,0:T(4,128)(2,1)S(1)}, bf16[8,4,512]{2,1,0:T(4,128)(2,1)S(1)}, u32[]{:S(2)}, u32[]{:S(2)}) collective-permute-start(bf16[8,4,512]{2,1,0:T(4,128)(2,1)S(1)} %dynamic-slice_bitcast_fusion.1), channel_id=1, source_target_pairs={{0,4},{4,0},{8,12},{12,8},{16,20},{20,16},{24,28},{28,24},{1,5},{5... | collective-permute-start | bytes 98312 | tf_op jit(solution)/shard_map/ppermute | solution.py:375
  48.3 1.3 %collective-permute-start.3 = (bf16[8,4,512]{2,1,0:T(4,128)(2,1)S(1)}, bf16[8,4,512]{2,1,0:T(4,128)(2,1)S(1)}, u32[]{:S(2)}, u32[]{:S(2)}) collective-permute-start(bf16[8,4,512]{2,1,0:T(4,128)(2,1)S(1)} %dynamic-slice_bitcast_fusion), channel_id=1, source_target_pairs={{0,4},{4,0},{8,12},{12,8},{16,20},{20,16},{24,28},{28,24},{1,5},{5... | collective-permute-start | bytes 98312 | tf_op jit(solution)/shard_map/ppermute | solution.py:375

commit v6 on v5

--- a/solution.py
+++ b/solution.py
@@ -68,7 +68,7 @@
         ((steps_hbm, steps_ref), (wi_hbm, wi_in), (wo_hbm, wo_in), (table_hbm, table_ref)))]
     taps = {(n, dc): [pltpu.make_async_copy(src.at[3 * dr + dc], dst.at[3 * dr + dc], sems.at[10 + 9 * n + 3 * dc + dr])
                       for dr in range(3)] for n, (src, dst) in enumerate(((w1_hbm, w1), (w2_hbm, w2))) for dc in range(3)}
-    for load in loads + sum(taps.values(), []):
+    for load in loads + sum(taps.values(), [])[:9]:
         load.start()
     blocks = scale_hbm.shape[1] // COLS
     loads[0].wait()
@@ -78,7 +78,7 @@
     for n, src in enumerate((scale_hbm, shift_hbm)):
         columns.append(pltpu.make_async_copy(src.at[:, pl.ds(begin, COLS)], block.at[n], sems.at[4 + 2 * n]))
         columns.append(pltpu.make_async_copy(src.at[:, blocks * COLS:], tail.at[n], sems.at[5 + 2 * n]))
-    for load in columns:
+    for load in columns + sum(taps.values(), [])[9:]:
         load.start()
     chan, lat = w1.shape[1], wi_in.shape[1]
     slot = lax.axis_index("tm")
@@ -91,11 +91,14 @@
         wo_rows[t * TAP_ROWS:t * TAP_ROWS + lat] = wo_in[t].astype(F32)
     wi_ref[...] = jnp.transpose(wi_rows[...])[:chan].astype(BF)
     wo_ref[...] = wo_rows[...].astype(BF)
-    for n, (w, u) in enumerate(((w1, u1), (w2, u2))):
+
+    def transform(n, w, u):
         for dc, work in enumerate(weight_pieces(w, u)):
             for load in taps[n, dc]:
                 load.wait()
             work()
+
+    transform(0, w1, u1)
     for load in loads[3:] + columns:
         load.wait()
     write_factors(factors, owner_ref, steps_ref, table_ref, slot, slots)
@@ -106,6 +109,7 @@
             part = jnp.sum(jnp.where(chosen, ref[n], 0.0), axis=1, keepdims=True)
             column = part if column is None else column + part
         dst[...] = jnp.broadcast_to(0.5 * (column + add), dst.shape)
+    transform(1, w2, u2)
 
 
 def prep_call(slots, chan, scalars, given):
@@ -158,6 +162,9 @@
             total = term if total is None else total + term
         return total
 
+    if not first:
+        here = [weighed(sent_ref.at[space], i) for i in range(HALO)]
+        there = [weighed(other_ref, i) for i in range(HALO)]
     for k, own in enumerate(own_rows):
         value = own
         if not first:
@@ -167,8 +174,7 @@
             elif row >= rows:
                 total = masked(weighed(sent_ref.at[jnp.minimum(space + 1, spaces - 1)], row - rows), row)
             else:
-                here, there = weighed(sent_ref.at[space], row % HALO), weighed(other_ref, row % HALO)
-                total = jnp.where(first_core == (row < HALO), here, there)
+                total = jnp.where(first_core == (row < HALO), here[row % HALO], there[row % HALO])
             value = total + factors[2 * slots, :lat] * own
         state[:, k * COLS:(k + 1) * COLS] = value.astype(BF).astype(F32)
 

time: 65.1 us -> 65.1 us (level)
  no operation moved by 1% of the time
where the time goes in v6:
time: 65.1 us; the launch traced here: 64.7 us
  blocking collectives  29.6 us (45%)
  Pallas kernels  23.9 us (37%)
  starting transfers between devices  7.12 us (11%)
  waiting for transfers between devices  1.99 us (3%)
  between operations  1.36 us (2%)
  other arithmetic  0.8 us (1%)
    all_to_all x2, blocking collectives, body(): lax.all_to_all(drift, ('space', 'tm'), 0, 0)  21.6 us
    pallas_call x3, Pallas kernels, drift_call(): pl.pallas_call(functools.partial(drift_kernel, first, last, copies, slots...  19.6 us
    all_to_all x1, blocking collectives, body(): sent = lax.all_to_all(drift, 'tm', 0, 0)  7.92 us
    ppermute x1, starting transfers between devices, neighbour_rows(): lax.ppermute(one, 'space', swap(0))  5.91 us
    pallas_call x1, Pallas kernels, prep_call(): pl.pallas_call(functools.partial(prep_kernel, slots), out_shape=[V((chan,...  3.53 us
    ppermute x2, waiting for transfers between devices, body(): sent = (sent, lax.ppermute(half, 'tm', [(t, t ^ 1) for t in range(slots)]))  1.98 us
  transfers between devices with their start and end apart: 4, of which 2 were waited for; matrix products, arithmetic and copies ran while one was open for 0% of the time, Pallas kernels for 5%

profile of v6, /device:TPU:0, one launch (start us, length us, event | category | flops | bytes accessed | tf_op | source)
XLA Modules:
  0.0 64.7 jit_solution(2918647118183520572)
XLA Ops:
  0.6 0.8 %slice_select_fusion = (f32[4,4,128]{2,1,0:T(4,128)S(1)}, f32[4,4,128]{2,1,0:T(4,128)S(1)}) fusion(f32[4,8,128]{2,1,0:T(8,128)} %bitcast.17, pred[]{:T(512)S(6)} %eq.5), kind=kLoop, calls=%fused_computation.2 | loop fusion | flops 4096 | bytes 32769 | tf_op jit(solution)/shard_map/jit(_where)/select_n | solution.py:361
  1.4 0.6 %collective-permute-start.1 = (f32[4,4,128]{2,1,0:T(4,128)S(1)}, f32[4,4,128]{2,1,0:T(4,128)S(1)}, u32[]{:S(2)}, u32[]{:S(2)}) collective-permute-start(f32[4,4,128]{2,1,0:T(4,128)S(1)} %get-tuple-element.24.sent_two), channel_id=1, source_target_pairs={{1,2},{2,1},{5,6},{6,5},{9,10},{10,9},{13,14},{14,13},{17,18},{18,... | collective-permute-start | bytes 24584 | tf_op jit(solution)/shard_map/ppermute | solution.py:362
  2.1 5.9 %collective-permute-start = (f32[4,4,128]{2,1,0:T(4,128)S(1)}, f32[4,4,128]{2,1,0:T(4,128)S(1)}, u32[]{:S(2)}, u32[]{:S(2)}) collective-permute-start(f32[4,4,128]{2,1,0:T(4,128)S(1)} %get-tuple-element.25.sent_one), channel_id=1, source_target_pairs={{0,1},{1,0},{2,3},{3,2},{4,5},{5,4},{6,7},{7,6},{8,9},{9,8},{10,11... | collective-permute-start | bytes 24584 | tf_op jit(solution)/shard_map/ppermute | solution.py:362
  8.7 3.5 %prep.1 = (f32[320,128]{1,0:T(8,128)S(1)}, f32[320,128]{1,0:T(8,128)S(1)}, bf16[320,128]{1,0:T(8,128)(2,1)S(1)}, bf16[72,320]{1,0:T(8,128)(2,1)S(1)}, f32[19,8,1...) custom-call(s32[1]{0:T(128)S(6)} %copy.12.owner_ref, s32[8]{0:T(128)} %steps_hbm.1, ...), custom_call_target="tpu_custom_call" | custom-call | flops 1048576 | bytes 8388608 | tf_op jit(solution)/shard_map/prep/pallas_call | solution.py:120
  12.2 0.0 collective-permute-done.1.got_two
  12.2 0.0 collective-permute-done.got_one
  12.2 6.5 %drift.3 = bf16[32,4,512]{2,1,0:T(4,128)(2,1)S(1)} custom-call(f32[4,4,128]{2,1,0:T(4,128)S(1)} %get-tuple-element.25.sent_one, f32[4,4,128]{2,1,0:T(4,128)S(1)} %get-tuple-element.24.sent_two, f32[4,4,128]{2,1,0:T(4,128)S(1)} %collective-permute-done.got_one, f32[4,4,128]{2,1,0:T(4,128)S(1)} %collective-permute-done.1.got_two, ...), custom_call_target="tpu_custom_call" | custom-call | flops 3460300800 | bytes 6291456 | tf_op jit(solution)/shard_map/drift/pallas_call | solution.py:328
  18.8 11.6 %all_to_all.15 = bf16[32,4,512]{2,1,0:T(4,128)(2,1)S(1)} all-to-all(bf16[32,4,512]{2,1,0:T(4,128)(2,1)S(1)} %drift.3), channel_id=1, replica_groups=mesh['tm'=8,'space'=4] {'space','tm'}, dimensions={0} | all-to-all | bytes 262144 | tf_op jit(solution)/shard_map/all_to_all | solution.py:379
  30.4 0.3 collective-permute-start.2
  30.7 1.0 %collective-permute-done.2.refs_1_ = bf16[8,4,512]{2,1,0:T(4,128)(2,1)S(1)} collective-permute-done((bf16[8,4,512]{2,1,0:T(4,128)(2,1)S(1)}, bf16[8,4,512]{2,1,0:T(4,128)(2,1)S(1)}, u32[]{:S(2)}, u32[]{:S(2)}) %collective-permute-start.2) | collective-permute-done | bytes 32800 | tf_op jit(solution)/shard_map/ppermute | solution.py:381
  31.7 6.6 %drift.4 = bf16[32,4,512]{2,1,0:T(4,128)(2,1)S(1)} custom-call(f32[4,4,128]{2,1,0:T(4,128)S(1)} %get-tuple-element.25.sent_one, f32[4,4,128]{2,1,0:T(4,128)S(1)} %get-tuple-element.24.sent_two, f32[4,4,128]{2,1,0:T(4,128)S(1)} %collective-permute-done.got_one, f32[4,4,128]{2,1,0:T(4,128)S(1)} %collective-permute-done.1.got_two, ...), custom_call_target="tpu_custom_call" | custom-call | flops 3460300800 | bytes 6291456 | tf_op jit(solution)/shard_map/drift/pallas_call | solution.py:328
  38.2 10.0 %all_to_all.16 = bf16[32,4,512]{2,1,0:T(4,128)(2,1)S(1)} all-to-all(bf16[32,4,512]{2,1,0:T(4,128)(2,1)S(1)} %drift.4), channel_id=1, replica_groups=mesh['tm'=8,'space'=4] {'space','tm'}, dimensions={0} | all-to-all | bytes 262144 | tf_op jit(solution)/shard_map/all_to_all | solution.py:379
  48.3 0.3 collective-permute-start.3
  48.5 1.0 %collective-permute-done.3.refs_1_ = bf16[8,4,512]{2,1,0:T(4,128)(2,1)S(1)} collective-permute-done((bf16[8,4,512]{2,1,0:T(4,128)(2,1)S(1)}, bf16[8,4,512]{2,1,0:T(4,128)(2,1)S(1)}, u32[]{:S(2)}, u32[]{:S(2)}) %collective-permute-start.3) | collective-permute-done | bytes 32800 | tf_op jit(solution)/shard_map/ppermute | solution.py:381
  49.5 6.5 %drift.5 = bf16[8,2,4,1024]{3,2,1,0:T(4,128)(2,1)S(1)} custom-call(f32[4,4,128]{2,1,0:T(4,128)S(1)} %get-tuple-element.25.sent_one, f32[4,4,128]{2,1,0:T(4,128)S(1)} %get-tuple-element.24.sent_two, f32[4,4,128]{2,1,0:T(4,128)S(1)} %collective-permute-done.got_one, f32[4,4,128]{2,1,0:T(4,128)S(1)} %collective-permute-done.1.got_two, ...), custom_call_target="tpu_custom_call" | custom-call | flops 3460300800 | bytes 6291456 | tf_op jit(solution)/shard_map/drift/pallas_call | solution.py:328
  56.1 7.9 %all_to_all.17.sent_ref = bf16[8,2,4,1024]{3,2,1,0:T(4,128)(2,1)S(1)} all-to-all(bf16[8,2,4,1024]{3,2,1,0:T(4,128)(2,1)S(1)} %drift.5), channel_id=1, replica_groups=mesh['tm'=8,'space'=4] {'tm'}, dimensions={0} | all-to-all | bytes 262144 | tf_op jit(solution)/shard_map/all_to_all | solution.py:383
  64.0 0.7 %finish.1 = (f32[1,4,8,128]{3,2,1,0:T(8,128)}, f32[4,8,128]{2,1,0:T(8,128)}) custom-call(f32[4,4,128]{2,1,0:T(4,128)S(1)} %get-tuple-element.25.sent_one, f32[4,4,128]{2,1,0:T(4,128)S(1)} %get-tuple-element.24.sent_two, bf16[8,2,4,1024]{3,2,1,0:T(4,128)(2,1)S(1)} %all_to_all.17.sent_ref, f32[19,8,128]{2,1,0:T(8,128)S(1)} %get-tuple-element.17.refs_4_.refs_6_.factors), custom_call_target="tpu_custom_call" | custom-call | tf_op jit(solution)/shard_map/finish/pallas_call | solution.py:384
  (2 shorter events, 0.0 us)
Async XLA Ops:
  1.4 10.8 %collective-permute-start.1 = (f32[4,4,128]{2,1,0:T(4,128)S(1)}, f32[4,4,128]{2,1,0:T(4,128)S(1)}, u32[]{:S(2)}, u32[]{:S(2)}) collective-permute-start(f32[4,4,128]{2,1,0:T(4,128)S(1)} %get-tuple-element.24.sent_two), channel_id=1, source_target_pairs={{1,2},{2,1},{5,6},{6,5},{9,10},{10,9},{13,14},{14,13},{17,18},{18,... | collective-permute-start | bytes 24584 | tf_op jit(solution)/shard_map/ppermute | solution.py:362
  2.1 10.1 %collective-permute-start = (f32[4,4,128]{2,1,0:T(4,128)S(1)}, f32[4,4,128]{2,1,0:T(4,128)S(1)}, u32[]{:S(2)}, u32[]{:S(2)}) collective-permute-start(f32[4,4,128]{2,1,0:T(4,128)S(1)} %get-tuple-element.25.sent_one), channel_id=1, source_target_pairs={{0,1},{1,0},{2,3},{3,2},{4,5},{5,4},{6,7},{7,6},{8,9},{9,8},{10,11... | collective-permute-start | bytes 24584 | tf_op jit(solution)/shard_map/ppermute | solution.py:362
  30.4 1.3 %collective-permute-start.2 = (bf16[8,4,512]{2,1,0:T(4,128)(2,1)S(1)}, bf16[8,4,512]{2,1,0:T(4,128)(2,1)S(1)}, u32[]{:S(2)}, u32[]{:S(2)}) collective-permute-start(bf16[8,4,512]{2,1,0:T(4,128)(2,1)S(1)} %dynamic-slice_bitcast_fusion.1), channel_id=1, source_target_pairs={{0,4},{4,0},{8,12},{12,8},{16,20},{20,16},{24,28},{28,24},{1,5},{5... | collective-permute-start | bytes 98312 | tf_op jit(solution)/shard_map/ppermute | solution.py:381
  48.3 1.3 %collective-permute-start.3 = (bf16[8,4,512]{2,1,0:T(4,128)(2,1)S(1)}, bf16[8,4,512]{2,1,0:T(4,128)(2,1)S(1)}, u32[]{:S(2)}, u32[]{:S(2)}) collective-permute-start(bf16[8,4,512]{2,1,0:T(4,128)(2,1)S(1)} %dynamic-slice_bitcast_fusion), channel_id=1, source_target_pairs={{0,4},{4,0},{8,12},{12,8},{16,20},{20,16},{24,28},{28,24},{1,5},{5... | collective-permute-start | bytes 98312 | tf_op jit(solution)/shard_map/ppermute | solution.py:381

commit v7 on v6

--- a/solution.py
+++ b/solution.py
@@ -260,7 +260,7 @@
             first_layer(ready)
             ready += 1
         beside = list(waiting)
-        for j in range(ready, min(pairs[-1] + 4, pairs_one + 1)):
+        for j in range(ready, min(pairs[-1] + 5, pairs_one + 1)):
             beside.append(functools.partial(first_layer, j))
             ready = j + 1
         conv(act_a, u1, pairs, beside, slot)

time: 65.1 us -> 64.7 us (level)
  no operation moved by 1% of the time
where the time goes in v7:
time: 64.7 us; the launch traced here: 64.3 us
  blocking collectives  29.6 us (46%)
  Pallas kernels  23.4 us (36%)
  starting transfers between devices  7.12 us (11%)
  waiting for transfers between devices  1.99 us (3%)
  between operations  1.36 us (2%)
  other arithmetic  0.8 us (1%)
    all_to_all x2, blocking collectives, body(): lax.all_to_all(drift, ('space', 'tm'), 0, 0)  21.6 us
    pallas_call x3, Pallas kernels, drift_call(): pl.pallas_call(functools.partial(drift_kernel, first, last, copies, slots...  19.2 us
    all_to_all x1, blocking collectives, body(): sent = lax.all_to_all(drift, 'tm', 0, 0)  7.92 us
    ppermute x1, starting transfers between devices, neighbour_rows(): lax.ppermute(one, 'space', swap(0))  5.91 us
    pallas_call x1, Pallas kernels, prep_call(): pl.pallas_call(functools.partial(prep_kernel, slots), out_shape=[V((chan,...  3.53 us
    ppermute x2, waiting for transfers between devices, body(): sent = (sent, lax.ppermute(half, 'tm', [(t, t ^ 1) for t in range(slots)]))  1.98 us
  transfers between devices with their start and end apart: 4, of which 2 were waited for; matrix products, arithmetic and copies ran while one was open for 0% of the time, Pallas kernels for 5%

profile of v7, /device:TPU:0, one launch (start us, length us, event | category | flops | bytes accessed | tf_op | source)
XLA Modules:
  0.0 64.3 jit_solution(8395576600914249056)
XLA Ops:
  0.6 0.8 %slice_select_fusion = (f32[4,4,128]{2,1,0:T(4,128)S(1)}, f32[4,4,128]{2,1,0:T(4,128)S(1)}) fusion(f32[4,8,128]{2,1,0:T(8,128)} %bitcast.17, pred[]{:T(512)S(6)} %eq.5), kind=kLoop, calls=%fused_computation.2 | loop fusion | flops 4096 | bytes 32769 | tf_op jit(solution)/shard_map/jit(_where)/select_n | solution.py:361
  1.4 0.6 %collective-permute-start.1 = (f32[4,4,128]{2,1,0:T(4,128)S(1)}, f32[4,4,128]{2,1,0:T(4,128)S(1)}, u32[]{:S(2)}, u32[]{:S(2)}) collective-permute-start(f32[4,4,128]{2,1,0:T(4,128)S(1)} %get-tuple-element.24.sent_two), channel_id=1, source_target_pairs={{1,2},{2,1},{5,6},{6,5},{9,10},{10,9},{13,14},{14,13},{17,18},{18,... | collective-permute-start | bytes 24584 | tf_op jit(solution)/shard_map/ppermute | solution.py:362
  2.1 5.9 %collective-permute-start = (f32[4,4,128]{2,1,0:T(4,128)S(1)}, f32[4,4,128]{2,1,0:T(4,128)S(1)}, u32[]{:S(2)}, u32[]{:S(2)}) collective-permute-start(f32[4,4,128]{2,1,0:T(4,128)S(1)} %get-tuple-element.25.sent_one), channel_id=1, source_target_pairs={{0,1},{1,0},{2,3},{3,2},{4,5},{5,4},{6,7},{7,6},{8,9},{9,8},{10,11... | collective-permute-start | bytes 24584 | tf_op jit(solution)/shard_map/ppermute | solution.py:362
  8.7 3.5 %prep.1 = (f32[320,128]{1,0:T(8,128)S(1)}, f32[320,128]{1,0:T(8,128)S(1)}, bf16[320,128]{1,0:T(8,128)(2,1)S(1)}, bf16[72,320]{1,0:T(8,128)(2,1)S(1)}, f32[19,8,1...) custom-call(s32[1]{0:T(128)S(6)} %copy.12.owner_ref, s32[8]{0:T(128)} %steps_hbm.1, ...), custom_call_target="tpu_custom_call" | custom-call | flops 1048576 | bytes 8388608 | tf_op jit(solution)/shard_map/prep/pallas_call | solution.py:120
  12.2 0.0 collective-permute-done.1.got_two
  12.2 0.0 collective-permute-done.got_one
  12.2 6.4 %drift.3 = bf16[32,4,512]{2,1,0:T(4,128)(2,1)S(1)} custom-call(f32[4,4,128]{2,1,0:T(4,128)S(1)} %get-tuple-element.25.sent_one, f32[4,4,128]{2,1,0:T(4,128)S(1)} %get-tuple-element.24.sent_two, f32[4,4,128]{2,1,0:T(4,128)S(1)} %collective-permute-done.got_one, f32[4,4,128]{2,1,0:T(4,128)S(1)} %collective-permute-done.1.got_two, ...), custom_call_target="tpu_custom_call" | custom-call | flops 3460300800 | bytes 6291456 | tf_op jit(solution)/shard_map/drift/pallas_call | solution.py:328
  18.6 11.6 %all_to_all.15 = bf16[32,4,512]{2,1,0:T(4,128)(2,1)S(1)} all-to-all(bf16[32,4,512]{2,1,0:T(4,128)(2,1)S(1)} %drift.3), channel_id=1, replica_groups=mesh['tm'=8,'space'=4] {'space','tm'}, dimensions={0} | all-to-all | bytes 262144 | tf_op jit(solution)/shard_map/all_to_all | solution.py:379
  30.3 0.3 collective-permute-start.2
  30.5 1.0 %collective-permute-done.2.refs_1_ = bf16[8,4,512]{2,1,0:T(4,128)(2,1)S(1)} collective-permute-done((bf16[8,4,512]{2,1,0:T(4,128)(2,1)S(1)}, bf16[8,4,512]{2,1,0:T(4,128)(2,1)S(1)}, u32[]{:S(2)}, u32[]{:S(2)}) %collective-permute-start.2) | collective-permute-done | bytes 32800 | tf_op jit(solution)/shard_map/ppermute | solution.py:381
  31.5 6.4 %drift.4 = bf16[32,4,512]{2,1,0:T(4,128)(2,1)S(1)} custom-call(f32[4,4,128]{2,1,0:T(4,128)S(1)} %get-tuple-element.25.sent_one, f32[4,4,128]{2,1,0:T(4,128)S(1)} %get-tuple-element.24.sent_two, f32[4,4,128]{2,1,0:T(4,128)S(1)} %collective-permute-done.got_one, f32[4,4,128]{2,1,0:T(4,128)S(1)} %collective-permute-done.1.got_two, ...), custom_call_target="tpu_custom_call" | custom-call | flops 3460300800 | bytes 6291456 | tf_op jit(solution)/shard_map/drift/pallas_call | solution.py:328
  38.0 10.0 %all_to_all.16 = bf16[32,4,512]{2,1,0:T(4,128)(2,1)S(1)} all-to-all(bf16[32,4,512]{2,1,0:T(4,128)(2,1)S(1)} %drift.4), channel_id=1, replica_groups=mesh['tm'=8,'space'=4] {'space','tm'}, dimensions={0} | all-to-all | bytes 262144 | tf_op jit(solution)/shard_map/all_to_all | solution.py:379
  48.0 0.3 collective-permute-start.3
  48.3 1.0 %collective-permute-done.3.refs_1_ = bf16[8,4,512]{2,1,0:T(4,128)(2,1)S(1)} collective-permute-done((bf16[8,4,512]{2,1,0:T(4,128)(2,1)S(1)}, bf16[8,4,512]{2,1,0:T(4,128)(2,1)S(1)}, u32[]{:S(2)}, u32[]{:S(2)}) %collective-permute-start.3) | collective-permute-done | bytes 32800 | tf_op jit(solution)/shard_map/ppermute | solution.py:381
  49.2 6.4 %drift.5 = bf16[8,2,4,1024]{3,2,1,0:T(4,128)(2,1)S(1)} custom-call(f32[4,4,128]{2,1,0:T(4,128)S(1)} %get-tuple-element.25.sent_one, f32[4,4,128]{2,1,0:T(4,128)S(1)} %get-tuple-element.24.sent_two, f32[4,4,128]{2,1,0:T(4,128)S(1)} %collective-permute-done.got_one, f32[4,4,128]{2,1,0:T(4,128)S(1)} %collective-permute-done.1.got_two, ...), custom_call_target="tpu_custom_call" | custom-call | flops 3460300800 | bytes 6291456 | tf_op jit(solution)/shard_map/drift/pallas_call | solution.py:328
  55.7 7.9 %all_to_all.17.sent_ref = bf16[8,2,4,1024]{3,2,1,0:T(4,128)(2,1)S(1)} all-to-all(bf16[8,2,4,1024]{3,2,1,0:T(4,128)(2,1)S(1)} %drift.5), channel_id=1, replica_groups=mesh['tm'=8,'space'=4] {'tm'}, dimensions={0} | all-to-all | bytes 262144 | tf_op jit(solution)/shard_map/all_to_all | solution.py:383
  63.6 0.7 %finish.1 = (f32[1,4,8,128]{3,2,1,0:T(8,128)}, f32[4,8,128]{2,1,0:T(8,128)}) custom-call(f32[4,4,128]{2,1,0:T(4,128)S(1)} %get-tuple-element.25.sent_one, f32[4,4,128]{2,1,0:T(4,128)S(1)} %get-tuple-element.24.sent_two, bf16[8,2,4,1024]{3,2,1,0:T(4,128)(2,1)S(1)} %all_to_all.17.sent_ref, f32[19,8,128]{2,1,0:T(8,128)S(1)} %get-tuple-element.17.refs_4_.refs_6_.factors), custom_call_target="tpu_custom_call" | custom-call | tf_op jit(solution)/shard_map/finish/pallas_call | solution.py:384
  (2 shorter events, 0.0 us)
Async XLA Ops:
  1.4 10.8 %collective-permute-start.1 = (f32[4,4,128]{2,1,0:T(4,128)S(1)}, f32[4,4,128]{2,1,0:T(4,128)S(1)}, u32[]{:S(2)}, u32[]{:S(2)}) collective-permute-start(f32[4,4,128]{2,1,0:T(4,128)S(1)} %get-tuple-element.24.sent_two), channel_id=1, source_target_pairs={{1,2},{2,1},{5,6},{6,5},{9,10},{10,9},{13,14},{14,13},{17,18},{18,... | collective-permute-start | bytes 24584 | tf_op jit(solution)/shard_map/ppermute | solution.py:362
  2.1 10.1 %collective-permute-start = (f32[4,4,128]{2,1,0:T(4,128)S(1)}, f32[4,4,128]{2,1,0:T(4,128)S(1)}, u32[]{:S(2)}, u32[]{:S(2)}) collective-permute-start(f32[4,4,128]{2,1,0:T(4,128)S(1)} %get-tuple-element.25.sent_one), channel_id=1, source_target_pairs={{0,1},{1,0},{2,3},{3,2},{4,5},{5,4},{6,7},{7,6},{8,9},{9,8},{10,11... | collective-permute-start | bytes 24584 | tf_op jit(solution)/shard_map/ppermute | solution.py:362
  30.3 1.3 %collective-permute-start.2 = (bf16[8,4,512]{2,1,0:T(4,128)(2,1)S(1)}, bf16[8,4,512]{2,1,0:T(4,128)(2,1)S(1)}, u32[]{:S(2)}, u32[]{:S(2)}) collective-permute-start(bf16[8,4,512]{2,1,0:T(4,128)(2,1)S(1)} %dynamic-slice_bitcast_fusion.1), channel_id=1, source_target_pairs={{0,4},{4,0},{8,12},{12,8},{16,20},{20,16},{24,28},{28,24},{1,5},{5... | collective-permute-start | bytes 98312 | tf_op jit(solution)/shard_map/ppermute | solution.py:381
  48.0 1.3 %collective-permute-start.3 = (bf16[8,4,512]{2,1,0:T(4,128)(2,1)S(1)}, bf16[8,4,512]{2,1,0:T(4,128)(2,1)S(1)}, u32[]{:S(2)}, u32[]{:S(2)}) collective-permute-start(bf16[8,4,512]{2,1,0:T(4,128)(2,1)S(1)} %dynamic-slice_bitcast_fusion), channel_id=1, source_target_pairs={{0,4},{4,0},{8,12},{12,8},{16,20},{20,16},{24,28},{28,24},{1,5},{5... | collective-permute-start | bytes 98312 | tf_op jit(solution)/shard_map/ppermute | solution.py:381
